TPU v7x, 512 devices: a whole 4x8x8 slice. The times are simulated.
512 devices in a mesh: ctx: 64 (over x, z, core), head: 8 (over y).
Axes of the slice: x: 4, y: 8, z: 8, core: 2. Of those that a mesh axis runs over, the one named last changes fastest.
Arguments:
- dec_states: bfloat16 [16384, 4096], P('ctx', 'head'), may hold values from -512 to 512
- norm_gain: float32 [4096], replicated, may hold values from 0.1 to 1.9
- w_query: bfloat16 [4096, 4096], P('ctx', 'head'), may hold values from -0.09375 to 0.09375
- enc_keys: bfloat16 [131072, 4096], P('ctx', 'head'), may hold values from -128 to 128
- enc_values: bfloat16 [131072, 4096], P('ctx', 'head'), may hold values from -24 to 24
- w_out: bfloat16 [4096, 4096], P('ctx', 'head'), may hold values from -0.09375 to 0.09375
- tgt_lengths: int32 [32], replicated, may hold values from 1 to 512, 8192 in all
- src_lengths: int32 [32], replicated, may hold values from 2049 to 4096, as said below
Outputs:
- attn_output: bfloat16 [16384, 4096], P('ctx', 'head')
Inputs may be any that keep to these rules, and one draw needn't show every extreme that they name: `tgt_lengths`: the lengths sum to 8192, and the longest equals 512. `src_lengths`: every example has more than 2048 encoder rows, and some example has all 4096.
All inputs are finite; a program needn't handle non-finite values.
Results may differ from a plain program's by a relative error of at most 0.009.
Values may be sent and summed in bfloat16 or wider, within the bound.
No kernel may reach another device: no remote copies, remote signals or barrier semaphores. Data moves between devices by JAX's collectives and lax.ppermute only.
A program may use at most 64 MiB of HBM per device.

v0:
```python
import jax
import jax.numpy as jnp
from jax import lax
from jax.sharding import PartitionSpec as P

DK = 64


def partner(value, axis, distance):
    mask = 2**distance
    pairs = [(source, source ^ mask) for source in range(lax.axis_size(axis))]
    return lax.ppermute(value, axis, pairs)


def attend(queries, keys, values, key_valid):
    row_count = queries.shape[0]
    head_count = queries.shape[1] // DK
    query_heads = jnp.moveaxis(queries.reshape(row_count, head_count, DK), 1, 0)
    key_heads = jnp.moveaxis(keys.reshape(-1, head_count, DK), 1, 0)
    value_heads = jnp.moveaxis(values.reshape(-1, head_count, DK), 1, 0)

    def one_head(head_items):
        query_head, key_head, value_head = head_items
        scores = jnp.dot(query_head, key_head.T, preferred_element_type=jnp.float32)
        scores = jnp.where(key_valid[None, :], scores, -jnp.inf)
        top_score = jnp.max(scores, axis=1)
        weights = jnp.exp(scores - top_score[:, None]).astype(jnp.bfloat16)
        totals = jnp.sum(weights.astype(jnp.float32), axis=1)
        weighted = jnp.dot(weights, value_head, preferred_element_type=jnp.float32)
        return (top_score, totals, weighted)

    top_score, totals, weighted = lax.map(one_head, (query_heads, key_heads, value_heads))
    return (top_score.T, totals.T, jnp.moveaxis(weighted, 0, 1).reshape(row_count, head_count * DK))


def combine_halves(first, second):
    top_one, totals_one, weighted_one = first
    top_two, totals_two, weighted_two = second
    row_count = weighted_one.shape[0]
    head_count = top_one.shape[1]
    largest = jnp.maximum(top_one, top_two)
    scale_one = jnp.exp(top_one - largest)
    scale_two = jnp.exp(top_two - largest)
    numer = (
        weighted_one.reshape(row_count, head_count, DK) * scale_one[:, :, None]
        + weighted_two.reshape(row_count, head_count, DK) * scale_two[:, :, None]
    )
    denom = totals_one * scale_one + totals_two * scale_two
    return (numer / denom[:, :, None]).reshape(row_count, head_count * DK)


def local(dec_states, norm_gain, w_query, enc_keys, enc_values, w_out, tgt_lengths, src_lengths):
    position = lax.axis_index("ctx")
    half_index = position % 2
    example = position // 2
    slot_ids = jnp.arange(tgt_lengths.shape[0], dtype=jnp.int32)
    tgt_len = jnp.sum(jnp.where(slot_ids == example, tgt_lengths, 0))
    src_len = jnp.sum(jnp.where(slot_ids == example, src_lengths, 0))
    enc_count = enc_keys.shape[0]
    full_states = lax.all_gather(dec_states, "head", axis=1, tiled=True)
    row_count = full_states.shape[0]
    states = full_states.astype(jnp.float32)
    normed = (
        states * lax.rsqrt(jnp.mean(states * states, axis=-1, keepdims=True) + 1e-06) * norm_gain
    ).astype(jnp.bfloat16)
    columns = normed
    queries = jnp.dot(
        columns,
        lax.all_gather(w_query, "ctx", axis=0, tiled=True),
        preferred_element_type=jnp.float32,
    ).astype(jnp.bfloat16)
    offsets = jnp.arange(enc_count, dtype=jnp.int32)
    own_valid = half_index * enc_count + offsets < src_len
    far_valid = (1 - half_index) * enc_count + offsets < src_len
    far_keys, far_values = partner((enc_keys, enc_values), "ctx", 0)
    nearby = attend(queries, enc_keys, enc_values, own_valid)
    distant = attend(queries, far_keys, far_values, far_valid)
    attended = combine_halves(nearby, distant)
    live_rows = half_index * row_count + jnp.arange(row_count, dtype=jnp.int32) < tgt_len
    attended = jnp.where(live_rows[:, None], attended, 0.0).astype(jnp.bfloat16)
    all_heads = lax.all_gather(attended, "head", axis=1, tiled=True)
    columns = all_heads
    projected = jnp.dot(
        columns,
        lax.all_gather(w_out, "ctx", axis=0, tiled=True),
        preferred_element_type=jnp.float32,
    )
    return projected.astype(jnp.bfloat16)


def solution(mesh):
    placed = (
        P("ctx", "head"),
        P(),
        P("ctx", "head"),
        P("ctx", "head"),
        P("ctx", "head"),
        P("ctx", "head"),
        P(),
        P(),
    )
    return jax.shard_map(
        local, mesh=mesh, in_specs=placed, out_specs=P("ctx", "head"), check_vma=False
    )
```

profile of v0, /device:TPU:6, one launch (start us, length us, event | category | flops | bytes accessed | tf_op | source)
XLA Modules:
  0.0 284.4 jit_solution(14177036345322470178)
XLA Ops:
  8.1 2.9 %copy.11 = bf16[2048,512]{0,1:T(8,128)(2,1)S(1)} copy(bf16[2048,512]{1,0:T(8,128)(2,1)} %param.15) | data formatting | bytes 4194304 | tf_op args[3]
  11.0 1.9 collective-permute-start
  12.9 4.0 %copy.12 = bf16[2048,512]{0,1:T(8,128)(2,1)} copy(bf16[2048,512]{1,0:T(8,128)(2,1)} %param.16) | data formatting | bytes 4194304 | tf_op args[4]
  16.9 2.5 collective-permute-start.1
  21.5 36.2 %all-gather.5.cloned.1.call-done = bf16[256,4096]{1,0:T(8,128)(2,1)} async-done(((bf16[256,512]{1,0:T(8,128)(2,1)}), bf16[256,4096]{1,0:T(8,128)(2,1)}) %all-gather.5.cloned.1.call-update) | async-done | bytes 2097168 | tf_op jit(solution)/shard_map/all_gather | solution.py:60
  57.7 2.1 fusion.22
  59.7 84.6 %all-gather.7.cloned.1.call-done = bf16[4096,512]{1,0:T(8,128)(2,1)} async-done(((bf16[64,512]{1,0:T(8,128)(2,1)}), bf16[4096,512]{1,0:T(8,128)(2,1)}) %all-gather.7.cloned.1.call-update) | async-done | bytes 4194320 | tf_op jit(solution)/shard_map/all_gather | solution.py:69
  144.3 4.1 %fusion.29 = bf16[256,512]{1,0:T(8,128)(2,1)S(1)} fusion(bf16[4096,512]{1,0:T(8,128)(2,1)} %all-gather.7.cloned.1.call-done, bf16[256,4096]{1,0:T(8,128)(2,1)} %all-gather.5.cloned.1.call-done, f32[4096]{0:T(1024)S(1)} %copy-done.1, f32[256]{0:T(256)S(1)} %add_rsqrt_fusion), kind=kOutput, calls=%fused_computation.38 | convolution fusion | flops 1078067200 | bytes 6571008 | tf_op jit(solution)/shard_map/dot_general | solution.py:67
  149.0 32.8 %while.31 = (s32[]{:T(128)}, f32[8,256]{1,0:T(8,128)S(1)}, f32[8,256]{1,0:T(8,128)S(1)}, f32[8,256,64]{1,2,0:T(8,128)S(1)}, bf16[8,256,64]{2,1,0:T(8,128)(2,1)S(...) while((s32[]{:T(128)}, f32[8,256]{1,0:T(8,128)S(1)}, ...), condition=%wide.region_10.11_spmd.clone, body=%wide.region_7.10_spmd.clone.sunk | while | flops 138415616 | bytes 6961277 | solution.py:32
  151.1 1.5 fusion.58
  155.2 1.5 fusion.58
  159.3 1.5 fusion.58
  167.4 1.5 fusion.58
  171.5 1.5 fusion.58
  179.7 1.5 fusion.58
  182.6 25.2 %while.30 = (s32[]{:T(128)}, f32[8,256]{1,0:T(8,128)S(1)}, f32[8,256]{1,0:T(8,128)S(1)}, f32[8,256,64]{1,2,0:T(8,128)S(1)}, bf16[8,256,64]{2,1,0:T(8,128)(2,1)S(...) while((s32[]{:T(128)}, f32[8,256]{1,0:T(8,128)S(1)}, ...), condition=%wide.region_6.7_spmd.clone, body=%wide.region_3.6_spmd.clone.sunk | while | flops 138415616 | bytes 6961277 | solution.py:32
  183.7 1.5 fusion.55
  190.0 1.5 fusion.55
  199.5 1.5 fusion.55
  202.7 1.5 fusion.55
  205.8 1.5 fusion.55
  209.8 19.8 %all-gather.11.cloned.1.call-done = bf16[4096,512]{1,0:T(8,128)(2,1)} async-done(((bf16[64,512]{1,0:T(8,128)(2,1)}), bf16[4096,512]{1,0:T(8,128)(2,1)}) %all-gather.11.cloned.1.call-update) | async-done | bytes 4194320 | tf_op jit(solution)/shard_map/all_gather | solution.py:85
  229.6 43.5 %all-gather.9.cloned.1.call-done = bf16[256,4096]{0,1:T(8,128)(2,1)} async-done(((bf16[256,512]{0,1:T(8,128)(2,1)}), bf16[256,4096]{0,1:T(8,128)(2,1)}) %all-gather.9.cloned.1.call-update) | async-done | bytes 2097168 | tf_op jit(solution)/shard_map/all_gather | solution.py:81
  273.1 4.8 %convolution_convert_fusion = bf16[256,512]{1,0:T(8,128)(2,1)} fusion(bf16[256,4096]{0,1:T(8,128)(2,1)} %all-gather.9.cloned.1.call-done, bf16[4096,512]{1,0:T(8,128)(2,1)} %all-gather.11.cloned.1.call-done), kind=kOutput, calls=%fused_computation.39 | convolution fusion | flops 1073872896 | bytes 6553600 | tf_op jit(solution)/shard_map/dot_general | solution.py:83
  (118 shorter events, 47.9 us)
Async XLA Ops:
  6.5 51.1 %all-gather.5.cloned.1.call-start = ((), (), s32[]{:S(2)}) async-start(), calls=%async_computation | async-start | bytes 2359296 | tf_op jit(solution)/shard_map/all_gather | solution.py:60
  7.3 137.1 %all-gather.7.cloned.1.call-start = ((), (), s32[]{:S(2)}) async-start(), calls=%async_computation.1 | async-start | bytes 4259840 | tf_op jit(solution)/shard_map/all_gather | solution.py:69
  8.0 221.6 %all-gather.11.cloned.1.call-start = ((), (), s32[]{:S(2)}) async-start(), calls=%async_computation.3 | async-start | bytes 4259840 | tf_op jit(solution)/shard_map/all_gather | solution.py:85
  11.0 8.6 %copy-start.2 = (s32[32]{0:T(128)S(1)}, s32[32]{0:T(128)}, u32[]{:S(2)}) copy-start(s32[32]{0:T(128)} %param.18) | copy-start | bytes 388
  11.0 9.8 %copy-start.3 = (s32[32]{0:T(128)S(1)}, s32[32]{0:T(128)}, u32[]{:S(2)}) copy-start(s32[32]{0:T(128)} %param.19) | copy-start | bytes 388
  11.0 137.9 %collective-permute-start = (bf16[2048,512]{0,1:T(8,128)(2,1)S(1)}, bf16[2048,512]{0,1:T(8,128)(2,1)}, u32[]{:S(2)}, u32[]{:S(2)}) collective-permute-start(bf16[2048,512]{0,1:T(8,128)(2,1)S(1)} %copy.11), channel_id=1, source_target_pairs={{0,8},{8,0},{16,24},{24,16},{32,40},{40,32},{48,56},{56,48},{64,72... | collective-permute-start | bytes 6291464 | tf_op jit(solution)/shard_map/ppermute | solution.py:12
  16.9 127.4 %copy-start.1 = (f32[4096]{0:T(1024)S(1)}, f32[4096]{0:T(1024)}, u32[]{:S(2)}) copy-start(f32[4096]{0:T(1024)} %param.13) | copy-start | bytes 49156
  16.9 132.0 %collective-permute-start.1 = (bf16[2048,512]{0,1:T(8,128)(2,1)}, bf16[2048,512]{0,1:T(8,128)(2,1)}, u32[]{:S(2)}, u32[]{:S(2)}) collective-permute-start(bf16[2048,512]{0,1:T(8,128)(2,1)} %copy.12), channel_id=1, source_target_pairs={{0,8},{8,0},{16,24},{24,16},{32,40},{40,32},{48,56},{56,48},{64,72... | collective-permute-start | bytes 6291464 | tf_op jit(solution)/shard_map/ppermute | solution.py:12
  19.5 253.6 %all-gather.9.cloned.1.call-start = ((), (), s32[]{:S(2)}) async-start(), calls=%async_computation.2 | async-start | bytes 2359296 | tf_op jit(solution)/shard_map/all_gather | solution.py:81
  181.7 0.8 copy-start
Sparse Core Ops, SparseCore 0:
  9.4 48.1 all-gather.4
  61.0 83.2 all-gather.6
  147.7 81.8 all-gather.10
  231.5 41.4 all-gather.8
where the time goes:
time: 286 us; the launch traced here: 284 us
  waiting for transfers between devices  185 us (65%)
  matrix products  48.1 us (17%)
  other arithmetic  22.9 us (8%)
  between operations  13.3 us (5%)
  local copies, waits for them, and re-layouts  9.48 us (3%)
  starting transfers between devices  4.57 us (2%)
    all_gather x1, waiting for transfers between devices, local(): lax.all_gather(w_query, 'ctx', axis=0, tiled=True)  84.6 us
    all_gather x1, waiting for transfers between devices, local(): all_heads = lax.all_gather(attended, 'head', axis=1, tiled=True)  43.5 us
    all_gather x1, waiting for transfers between devices, local(): full_states = lax.all_gather(dec_states, 'head', axis=1, tiled=True)  36.2 us
    dot_general x16, matrix products, one_head(): weighted = jnp.dot(weights, value_head, preferred_element_type=jnp.float32)  23.6 us
    all_gather x1, waiting for transfers between devices, local(): lax.all_gather(w_out, 'ctx', axis=0, tiled=True)  19.8 us
    dot_general x16, matrix products, one_head(): scores = jnp.dot(query_head, key_head.T, preferred_element_type=jnp.float32)  15.6 us
    unnamed x11, local copies, waits for them, and re-layouts  7.97 us
    reduce_sum x16, other arithmetic, one_head(): totals = jnp.sum(weights.astype(jnp.float32), axis=1)  6.98 us
  transfers between devices with their start and end apart: 6, of which 4 were waited for; matrix products, arithmetic and copies ran while one was open for 26% of the time, Pallas kernels for 0%

commit v1 on v0

v1 whole, which is shorter than its diff:
```python
import functools

import jax
import jax.numpy as jnp
from jax import lax
from jax.experimental import pallas as pl
from jax.experimental.pallas import tpu as pltpu
from jax.sharding import PartitionSpec as P

DK = 64
NX, NZ = 4, 8


def place(x, z, core):
    return ((x % NX) * NZ + z % NZ) * 2 + core


def along_x(shift):
    return [
        (place(x, z, core), place(x + shift, z, core))
        for x in range(NX)
        for z in range(NZ)
        for core in range(2)
    ]


PARTNERS = [(i, i ^ 1) for i in range(2 * NX * NZ)]
Z_GROUPS = [[place(x, z, core) for z in range(NZ)] for x in range(NX) for core in range(2)]
X_GROUPS = [[place(x, z, core) for x in range(NX)] for z in range(NZ) for core in range(2)]


def fill_weights(idx_ref, own_ref, far_ref, w, sems):
    copies = []
    for i in range(NX):
        copies.append(
            pltpu.make_async_copy(own_ref.at[i], w.at[idx_ref[i], :, idx_ref[NX]], sems.at[i])
        )
        copies.append(
            pltpu.make_async_copy(
                far_ref.at[i], w.at[idx_ref[i], :, 1 - idx_ref[NX]], sems.at[NX + i]
            )
        )
    return copies


def project_kernel(normalize, idx_ref, x_ref, gain_ref, own_ref, far_ref, o_ref, xs, w, sems):
    blocks, rows, width = xs.shape
    copies = fill_weights(idx_ref, own_ref, far_ref, w, sems)
    load = pltpu.make_async_copy(x_ref, xs, sems.at[2 * NX])
    load.start()
    for copy in copies:
        copy.start()
    load.wait()
    if normalize:
        square = jnp.zeros((rows, width), jnp.float32)
        for b in range(blocks):
            part = xs[b].astype(jnp.float32)
            square = square + part * part
        mean = jnp.sum(square, axis=1, keepdims=True) / (blocks * width)
        scale = lax.rsqrt(mean + 1e-06)
        for b in range(blocks):
            part = xs[b].astype(jnp.float32)
            xs[b] = (part * scale * gain_ref[b]).astype(jnp.bfloat16)
    for copy in copies:
        copy.wait()
    acc = jnp.zeros(o_ref.shape, jnp.float32)
    for b in range(blocks):
        depth = NZ * NX // blocks
        at = b * depth
        part = w[at // NZ, at % NZ : at % NZ + depth].reshape(width, o_ref.shape[1])
        acc = acc + jnp.dot(xs[b], part, preferred_element_type=jnp.float32)
    o_ref[...] = acc.astype(jnp.bfloat16)


def project(normalize, idx, x, gain, own, far):
    blocks, rows, width = x.shape
    piece = own.shape[2]
    out = own.shape[3]
    anywhere = pl.BlockSpec(memory_space=pl.ANY)
    return pl.pallas_call(
        functools.partial(project_kernel, normalize),
        out_shape=jax.ShapeDtypeStruct((rows, out), jnp.bfloat16),
        grid_spec=pltpu.PrefetchScalarGridSpec(
            num_scalar_prefetch=1,
            grid=(1,),
            in_specs=[
                anywhere,
                pl.BlockSpec((blocks, 1, width), lambda i, s: (0, 0, 0)),
                anywhere,
                anywhere,
            ],
            out_specs=pl.BlockSpec((rows, out), lambda i, s: (0, 0)),
            scratch_shapes=[
                pltpu.VMEM((blocks, rows, width), jnp.bfloat16),
                pltpu.VMEM((NX, NZ, 2, piece, out), jnp.bfloat16),
                pltpu.SemaphoreType.DMA((2 * NX + 1,)),
            ],
        ),
        compiler_params=pltpu.CompilerParams(vmem_limit_bytes=32 << 20),
        cost_estimate=pl.CostEstimate(
            flops=2 * rows * blocks * width * out,
            bytes_accessed=2 * blocks * width * (rows + out),
            transcendentals=0,
        ),
        name="project",
    )(idx, x, gain, own, far)


def attend_kernel(step, s_ref, q_ref, ko_ref, vo_ref, kf_ref, vf_ref, o_ref, keys, val_a, val_b):
    half = ko_ref.shape[0]
    rows = q_ref.shape[0]
    tile = 256
    first = lax.broadcasted_iota(jnp.int32, (1, 2 * DK), 1) < DK
    sides = ((0, ko_ref, vo_ref, s_ref[0]), (half, kf_ref, vf_ref, s_ref[1]))
    for base, k_ref, v_ref, count in sides:
        for c in range(0, half, tile):
            valid = lax.broadcasted_iota(jnp.int32, (tile, 1), 0) + c < count
            there = slice(base + c, base + c + tile)
            keys[there, :] = jnp.where(valid, k_ref[c : c + tile, :], k_ref[0:1, :])
            v = v_ref[c : c + tile, :]
            one, zero = jnp.ones_like(v), jnp.zeros_like(v)
            val_a[there, :] = jnp.where(valid, jnp.where(first, v, one), zero)
            val_b[there, :] = jnp.where(valid, jnp.where(first, one, v), zero)
    q = q_ref[...]
    parts = []
    for mine, values in ((first, val_a), (~first, val_b)):
        q_head = jnp.where(mine, q, jnp.zeros_like(q))
        top = acc = None
        for c in range(0, 2 * half, step):
            scores = lax.dot_general(
                q_head,
                keys[c : c + step, :],
                (((1,), (1,)), ((), ())),
                preferred_element_type=jnp.float32,
            )
            new_top = jnp.max(scores, axis=1, keepdims=True)
            if top is not None:
                new_top = jnp.maximum(top, new_top)
            weights = jnp.exp(scores - new_top).astype(jnp.bfloat16)
            part = jnp.dot(weights, values[c : c + step, :], preferred_element_type=jnp.float32)
            acc = part if top is None else acc * jnp.exp(top - new_top) + part
            top = new_top
        parts.append(acc / pltpu.roll(acc, DK, 1))
    live = lax.broadcasted_iota(jnp.int32, (rows, 1), 0) < s_ref[2]
    o_ref[...] = jnp.where(live, jnp.where(first, parts[0], parts[1]), 0.0).astype(jnp.bfloat16)


def attend(counts, q, own_k, own_v, far_k, far_v):
    rows, width = q.shape
    half = own_k.shape[0]
    pair = 2 * DK
    kv = pl.BlockSpec((half, pair), lambda h, s: (0, h))
    qs = pl.BlockSpec((rows, pair), lambda h, s: (0, h))
    return pl.pallas_call(
        functools.partial(attend_kernel, half),
        out_shape=jax.ShapeDtypeStruct((rows, width), jnp.bfloat16),
        grid_spec=pltpu.PrefetchScalarGridSpec(
            num_scalar_prefetch=1,
            grid=(width // pair,),
            in_specs=[qs, kv, kv, kv, kv],
            out_specs=qs,
            scratch_shapes=[pltpu.VMEM((2 * half, pair), jnp.bfloat16)] * 3,
        ),
        compiler_params=pltpu.CompilerParams(vmem_limit_bytes=40 << 20),
        cost_estimate=pl.CostEstimate(
            flops=16 * rows * width * half,
            bytes_accessed=8 * half * width,
            transcendentals=2 * rows * width // DK * half,
        ),
        name="attend",
    )(counts, q, own_k, own_v, far_k, far_v)


def local(dec_states, norm_gain, w_query, enc_keys, enc_values, w_out, tgt_lengths, src_lengths):
    heads = lax.axis_size("head")
    position = lax.axis_index("ctx")
    core = position % 2
    x = position // (2 * NZ)
    example = position // 2
    rows, width = dec_states.shape
    piece = w_query.shape[0]
    enc_count = enc_keys.shape[0]
    slot_ids = jnp.arange(tgt_lengths.shape[0], dtype=jnp.int32)
    tgt_len = jnp.sum(jnp.where(slot_ids == example, tgt_lengths, 0))
    src_len = jnp.sum(jnp.where(slot_ids == example, src_lengths, 0))
    counts = jnp.stack(
        [src_len - core * enc_count, src_len - (1 - core) * enc_count, tgt_len - core * rows]
    ).astype(jnp.int32)

    states = lax.all_gather(dec_states, "head")

    pieces = jnp.broadcast_to(
        jnp.concatenate([w_query, w_out], axis=1)[None], (NZ, piece, 2 * width)
    )
    pieces = lax.all_to_all(pieces, "ctx", 0, 0, axis_index_groups=Z_GROUPS)
    wq_own = pieces[:, :, :width].reshape(NZ * piece, width)
    wo_own = pieces[:, :, width:].reshape(NZ * piece, width)

    far_keys = lax.ppermute(enc_keys, "ctx", PARTNERS)
    far_values = lax.ppermute(enc_values, "ctx", PARTNERS)

    mid = NZ * piece // 2
    ahead = lax.ppermute(wq_own, "ctx", along_x(1))
    behind = lax.ppermute(wq_own, "ctx", along_x(-1))
    last_top = lax.ppermute(ahead[:mid], "ctx", along_x(1))
    last_low = lax.ppermute(behind[mid:], "ctx", along_x(-1))
    wq_core = jnp.concatenate([wq_own, ahead, behind, last_top, last_low], axis=0)
    wq_far = lax.ppermute(wq_core, "ctx", PARTNERS)

    wo_core = lax.all_gather(wo_own, "ctx", axis_index_groups=X_GROUPS)
    wo_core = wo_core.reshape(NX * NZ * piece, width)
    wo_far = lax.ppermute(wo_core, "ctx", PARTNERS)

    blocks = (NX, NZ, piece, width)
    ring = jnp.stack([x, (x - 1) % NX, (x + 1) % NX, (x + 2) % NX, core]).astype(jnp.int32)
    order = jnp.stack([0 * x, 0 * x + 1, 0 * x + 2, 0 * x + 3, core]).astype(jnp.int32)
    gain = norm_gain.reshape(heads, 1, width)
    queries = project(True, ring, states, gain, wq_core.reshape(blocks), wq_far.reshape(blocks))
    attended = attend(counts, queries, enc_keys, enc_values, far_keys, far_values)
    everything = lax.all_gather(attended, "head")
    return project(False, order, everything, gain, wo_core.reshape(blocks), wo_far.reshape(blocks))


def solution(mesh):
    placed = (
        P("ctx", "head"),
        P(),
        P("ctx", "head"),
        P("ctx", "head"),
        P("ctx", "head"),
        P("ctx", "head"),
        P(),
        P(),
    )
    return jax.shard_map(
        local, mesh=mesh, in_specs=placed, out_specs=P("ctx", "head"), check_vma=False
    )
```

time: 286 us -> 164 us (0.57)
  waiting for transfers between devices: 185 us -> 53 us
  matrix products: 48.1 us -> 0 us
  blocking collectives: 0 us -> 38.8 us
  Pallas kernels: 0 us -> 25.9 us
  other arithmetic: 22.9 us -> 1.67 us
  starting transfers between devices: 4.57 us -> 20.4 us
    all_gather x4 -> x3, waiting for transfers between devices: 184 us -> 34.1 us  [the longest x1 34.1 us: local(): everything = lax.all_gather(attended, 'head')]
    dot_general x34 -> x0, matrix products: 48.1 us -> none  [the longest x16 23.6 us: one_head(): weighted = jnp.dot(weights, value_head, preferred_element_type=jnp.float32)]
    all_to_all x0 -> x1, blocking collectives: none -> 38.8 us  [local(): pieces = lax.all_to_all(pieces, 'ctx', 0, 0, axis_index_groups=Z_GROUPS)]
    pallas_call x0 -> x3, Pallas kernels: none -> 25.9 us  [the longest x1 19.2 us: attend(): pl.pallas_call(functools.partial(attend_kernel, half), out_shape=jax.Shap...]
    ppermute x2 -> x8, waiting for transfers between devices: 0.01 us -> 18.1 us  [the longest x1 7.84 us: local(): ahead = lax.ppermute(wq_own, 'ctx', along_x(1))]
    ppermute x2 -> x8, starting transfers between devices: 4.45 us -> 20.3 us  [the longest x1 3.6 us: local(): last_top = lax.ppermute(ahead[:mid], 'ctx', along_x(1))]
    lt x17 -> x0, other arithmetic: 10.7 us -> none  [the longest x8 5.01 us: local(): far_valid = (1 - half_index) * enc_count + offsets < src_len]
    reduce_sum x18 -> x0, other arithmetic: 9.7 us -> none  [the longest x16 6.98 us: one_head(): totals = jnp.sum(weights.astype(jnp.float32), axis=1)]
  transfers between devices with their start and end apart: 6 -> 11, of which waited for: 4 -> 5; matrix products, arithmetic and copies ran while one was open for 26% -> 3% of each run, Pallas kernels for 0% -> 14%
where the time goes in v1:
time: 164 us; the launch traced here: 163 us
  waiting for transfers between devices  53 us (32%)
  blocking collectives  38.8 us (24%)
  Pallas kernels  25.9 us (16%)
  starting transfers between devices  20.4 us (12%)
  between operations  15.4 us (9%)
  local copies, waits for them, and re-layouts  8.17 us (5%)
  other arithmetic  1.67 us (1%)
    all_to_all x1, blocking collectives, local(): pieces = lax.all_to_all(pieces, 'ctx', 0, 0, axis_index_groups=Z_GROUPS)  38.8 us
    all_gather x1, waiting for transfers between devices, local(): everything = lax.all_gather(attended, 'head')  34.1 us
    pallas_call x1, Pallas kernels, attend(): pl.pallas_call(functools.partial(attend_kernel, half), out_shape=jax.Shap...  19.2 us
    ppermute x1, waiting for transfers between devices, local(): ahead = lax.ppermute(wq_own, 'ctx', along_x(1))  7.84 us
    pallas_call x2, Pallas kernels, project(): pl.pallas_call(functools.partial(project_kernel, normalize), out_shape=ja...  6.62 us
    ppermute x1, waiting for transfers between devices, local(): last_low = lax.ppermute(behind[mid:], 'ctx', along_x(-1))  6.17 us
    unnamed x16, local copies, waits for them, and re-layouts  5.97 us
    ppermute x1, waiting for transfers between devices, local(): wo_far = lax.ppermute(wo_core, 'ctx', PARTNERS)  3.89 us
  transfers between devices with their start and end apart: 11, of which 5 were waited for; matrix products, arithmetic and copies ran while one was open for 3% of the time, Pallas kernels for 14%

profile of v1, /device:TPU:6, one launch (start us, length us, event | category | flops | bytes accessed | tf_op | source)
XLA Modules:
  0.0 163.4 jit_solution(15550341071101912405)
XLA Ops:
  7.3 0.9 pad_maximum_fusion
  8.3 38.8 %all_to_all.5 = bf16[8,64,1024]{2,1,0:T(8,128)(2,1)S(1)} all-to-all(bf16[8,64,1024]{2,1,0:T(8,128)(2,1)S(1)} %broadcast_in_dim.12), channel_id=1, replica_groups={{0,16,32,48,64,80,96,112},{8,24,40,56,72,88,104,120},{128,144,160,176,1..., dimensions={0} | all-to-all | bytes 2097152 | tf_op jit(solution)/shard_map/all_to_all | solution.py:195
  47.2 0.9 fusion.2
  48.1 2.4 %collective-permute-start = (bf16[512,512]{1,0:T(8,128)(2,1)S(1)}, bf16[512,512]{1,0:T(8,128)(2,1)S(1)}, u32[]{:S(2)}, u32[]{:S(2)}) collective-permute-start(bf16[512,512]{1,0:T(8,128)(2,1)S(1)} %bitcast.27), channel_id=1, source_target_pairs={{0,128},{8,136},{16,144},{24,152},{32,160},{40,168},{48,176},{56,1... | collective-permute-start | bytes 1572872 | tf_op jit(solution)/shard_map/ppermute | solution.py:203
  50.4 3.5 %collective-permute-start.1 = (bf16[512,512]{1,0:T(8,128)(2,1)S(1)}, bf16[512,512]{1,0:T(8,128)(2,1)}, u32[]{:S(2)}, u32[]{:S(2)}) collective-permute-start(bf16[512,512]{1,0:T(8,128)(2,1)S(1)} %bitcast.28), channel_id=1, source_target_pairs={{0,384},{8,392},{16,400},{24,408},{32,416},{40,424},{48,432},{56,4... | collective-permute-start | bytes 1572872 | tf_op jit(solution)/shard_map/ppermute | solution.py:204
  54.0 7.8 %collective-permute-done = bf16[512,512]{1,0:T(8,128)(2,1)S(1)} collective-permute-done((bf16[512,512]{1,0:T(8,128)(2,1)S(1)}, bf16[512,512]{1,0:T(8,128)(2,1)S(1)}, u32[]{:S(2)}, u32[]{:S(2)}) %collective-permute-start) | collective-permute-done | bytes 524320 | tf_op jit(solution)/shard_map/ppermute | solution.py:203
  61.9 3.6 %collective-permute-start.2 = (bf16[256,512]{1,0:T(8,128)(2,1)S(1)}, bf16[256,512]{1,0:T(8,128)(2,1)S(1)}, u32[]{:S(2)}, u32[]{:S(2)}) collective-permute-start(bf16[256,512]{1,0:T(8,128)(2,1)S(1)} %slice.17), channel_id=1, source_target_pairs={{0,128},{8,136},{16,144},{24,152},{32,160},{40,168},{48,176},{56,1... | collective-permute-start | bytes 786440 | tf_op jit(solution)/shard_map/ppermute | solution.py:205
  65.5 1.0 slice.18
  66.5 2.2 %collective-permute-start.3 = (bf16[256,512]{1,0:T(8,128)(2,1)S(1)}, bf16[256,512]{1,0:T(8,128)(2,1)S(1)}, u32[]{:S(2)}, u32[]{:S(2)}) collective-permute-start(bf16[256,512]{1,0:T(8,128)(2,1)S(1)} %slice.18), channel_id=1, source_target_pairs={{0,384},{8,392},{16,400},{24,408},{32,416},{40,424},{48,432},{56,4... | collective-permute-start | bytes 786440 | tf_op jit(solution)/shard_map/ppermute | solution.py:206
  68.8 1.1 constant_dynamic-update-slice_fusion.2
  70.1 6.2 %collective-permute-done.3 = bf16[256,512]{1,0:T(8,128)(2,1)S(1)} collective-permute-done((bf16[256,512]{1,0:T(8,128)(2,1)S(1)}, bf16[256,512]{1,0:T(8,128)(2,1)S(1)}, u32[]{:S(2)}, u32[]{:S(2)}) %collective-permute-start.3) | collective-permute-done | bytes 262176 | tf_op jit(solution)/shard_map/ppermute | solution.py:206
  76.3 1.9 %collective-permute-start.4 = (bf16[2048,512]{1,0:T(8,128)(2,1)S(1)}, bf16[2048,512]{1,0:T(8,128)(2,1)}, u32[]{:S(2)}, u32[]{:S(2)}) collective-permute-start(bf16[2048,512]{1,0:T(8,128)(2,1)S(1)} %constant_dynamic-update-slice_fusion), channel_id=1, source_target_pairs={{0,8},{8,0},{16,24},{24,16},{32,40},{40,32},{48,56},{56,48},{64,72... | collective-permute-start | bytes 6291464 | tf_op jit(solution)/shard_map/ppermute | solution.py:208
  78.3 2.4 %collective-permute-start.5 = (bf16[2048,512]{1,0:T(8,128)(2,1)}, bf16[2048,512]{1,0:T(8,128)(2,1)}, u32[]{:S(2)}, u32[]{:S(2)}) collective-permute-start(bf16[2048,512]{1,0:T(8,128)(2,1)} %ko_ref.1), channel_id=1, source_target_pairs={{0,8},{8,0},{16,24},{24,16},{32,40},{40,32},{48,56},{56,48},{64,72... | collective-permute-start | bytes 6291464 | tf_op jit(solution)/shard_map/ppermute | solution.py:199
  80.7 1.9 %collective-permute-start.6 = (bf16[2048,512]{1,0:T(8,128)(2,1)}, bf16[2048,512]{1,0:T(8,128)(2,1)}, u32[]{:S(2)}, u32[]{:S(2)}) collective-permute-start(bf16[2048,512]{1,0:T(8,128)(2,1)} %vo_ref.1), channel_id=1, source_target_pairs={{0,8},{8,0},{16,24},{24,16},{32,40},{40,32},{48,56},{56,48},{64,72... | collective-permute-start | bytes 6291464 | tf_op jit(solution)/shard_map/ppermute | solution.py:200
  82.7 0.7 fusion
  85.6 1.6 copy-done.1
  87.2 3.6 %project.2.q_ref = bf16[256,512]{1,0:T(8,128)(2,1)S(1)} custom-call(s32[5]{0:T(128)S(1)} %stack.44.idx_ref, bf16[8,256,512]{2,1,0:T(8,128)(2,1)S(1)} %bitcast.21, f32[8,1,512]{2,1,0:T(1,128)S(1)} %bitcast.24, bf16[4,8,64,512]{3,2,1,0:T(8,128)(2,1)S(1)} %bitcast.18, bf16[4,8,64,512]{3,2,1,0:T(8,128)(2,1)} %bitcast.12.far_ref), custom_call_target="tpu_custom_call" | custom-call | flops 1073741824 | bytes 6291456 | tf_op jit(solution)/shard_map/project/pallas_call | solution.py:80
  90.8 19.2 %attend.1 = bf16[256,512]{1,0:T(8,128)(2,1)} custom-call(s32[3]{0:T(128)S(1)} %pad_add_fusion.s_ref, bf16[256,512]{1,0:T(8,128)(2,1)S(1)} %project.2.q_ref, bf16[2048,512]{1,0:T(8,128)(2,1)} %ko_ref.1, bf16[2048,512]{1,0:T(8,128)(2,1)} %vo_ref.1, bf16[2048,512]{1,0:T(8,128)(2,1)} %collective-permute-done.5.kf_ref, ...), custom_call_target="tpu_custom_call" | custom-call | flops 4294967296 | bytes 8388608 | tf_op jit(solution)/shard_map/attend/pallas_call | solution.py:154
  110.2 2.4 %collective-permute-start.7 = (bf16[2048,512]{1,0:T(8,128)(2,1)}, bf16[2048,512]{1,0:T(8,128)(2,1)S(1)}, u32[]{:S(2)}, u32[]{:S(2)}) collective-permute-start(bf16[2048,512]{1,0:T(8,128)(2,1)} %bitcast.19), channel_id=1, source_target_pairs={{0,8},{8,0},{16,24},{24,16},{32,40},{40,32},{48,56},{56,48},{64,72... | collective-permute-start | bytes 6291464 | tf_op jit(solution)/shard_map/ppermute | solution.py:212
  112.7 3.9 %collective-permute-done.7 = bf16[2048,512]{1,0:T(8,128)(2,1)S(1)} collective-permute-done((bf16[2048,512]{1,0:T(8,128)(2,1)}, bf16[2048,512]{1,0:T(8,128)(2,1)S(1)}, u32[]{:S(2)}, u32[]{:S(2)}) %collective-permute-start.7) | collective-permute-done | bytes 2097184 | tf_op jit(solution)/shard_map/ppermute | solution.py:212
  116.5 34.1 %all-gather.10.cloned.1.call-done = bf16[2048,512]{1,0:T(8,128)(2,1)} async-done(((bf16[256,512]{1,0:T(8,128)(2,1)}), bf16[2048,512]{1,0:T(8,128)(2,1)}) %all-gather.10.cloned.1.call-update) | async-done | bytes 2097168 | tf_op jit(solution)/shard_map/all_gather | solution.py:220
  150.6 1.6 copy-done
  152.2 1.6 copy-done.2
  153.8 3.0 %project.3 = bf16[256,512]{1,0:T(8,128)(2,1)} custom-call(s32[5]{0:T(128)S(1)} %stack.35.idx_ref, bf16[8,256,512]{2,1,0:T(8,128)(2,1)S(1)} %bitcast.22, f32[8,1,512]{2,1,0:T(1,128)S(1)} %bitcast.25, bf16[4,8,64,512]{3,2,1,0:T(8,128)(2,1)S(1)} %bitcast.20, bf16[4,8,64,512]{3,2,1,0:T(8,128)(2,1)S(1)} %bitcast.23), custom_call_target="tpu_custom_call" | custom-call | flops 1073741824 | bytes 6291456 | tf_op jit(solution)/shard_map/project/pallas_call | solution.py:80
  (31 shorter events, 1.6 us)
Async XLA Ops:
  6.5 79.1 %all-gather.8.cloned.1.call-start = ((), (), s32[]{:S(2)}) async-start(), calls=%async_computation.2 | async-start | bytes 2359296 | tf_op jit(solution)/shard_map/all_gather | solution.py:190
  7.3 102.9 %all-gather.6.cloned.1.call-start = ((), (), s32[]{:S(2)}) async-start(), calls=%async_computation.1 | async-start | bytes 2621440 | tf_op jit(solution)/shard_map/all_gather | solution.py:210
  48.1 13.8 %collective-permute-start = (bf16[512,512]{1,0:T(8,128)(2,1)S(1)}, bf16[512,512]{1,0:T(8,128)(2,1)S(1)}, u32[]{:S(2)}, u32[]{:S(2)}) collective-permute-start(bf16[512,512]{1,0:T(8,128)(2,1)S(1)} %bitcast.27), channel_id=1, source_target_pairs={{0,128},{8,136},{16,144},{24,152},{32,160},{40,168},{48,176},{56,1... | collective-permute-start | bytes 1572872 | tf_op jit(solution)/shard_map/ppermute | solution.py:203
  50.4 15.1 %collective-permute-start.1 = (bf16[512,512]{1,0:T(8,128)(2,1)S(1)}, bf16[512,512]{1,0:T(8,128)(2,1)}, u32[]{:S(2)}, u32[]{:S(2)}) collective-permute-start(bf16[512,512]{1,0:T(8,128)(2,1)S(1)} %bitcast.28), channel_id=1, source_target_pairs={{0,384},{8,392},{16,400},{24,408},{32,416},{40,424},{48,432},{56,4... | collective-permute-start | bytes 1572872 | tf_op jit(solution)/shard_map/ppermute | solution.py:204
  53.9 96.7 %all-gather.10.cloned.1.call-start = ((), (), s32[]{:S(2)}) async-start(), calls=%async_computation.3 | async-start | bytes 2359296 | tf_op jit(solution)/shard_map/all_gather | solution.py:220
  61.9 8.3 %collective-permute-start.2 = (bf16[256,512]{1,0:T(8,128)(2,1)S(1)}, bf16[256,512]{1,0:T(8,128)(2,1)S(1)}, u32[]{:S(2)}, u32[]{:S(2)}) collective-permute-start(bf16[256,512]{1,0:T(8,128)(2,1)S(1)} %slice.17), channel_id=1, source_target_pairs={{0,128},{8,136},{16,144},{24,152},{32,160},{40,168},{48,176},{56,1... | collective-permute-start | bytes 786440 | tf_op jit(solution)/shard_map/ppermute | solution.py:205
  65.5 17.2 %copy-start.4 = (s32[32]{0:T(128)S(1)}, s32[32]{0:T(128)}, u32[]{:S(2)}) copy-start(s32[32]{0:T(128)} %param.15) | copy-start | bytes 388
  65.5 17.2 %copy-start.5 = (s32[32]{0:T(128)S(1)}, s32[32]{0:T(128)}, u32[]{:S(2)}) copy-start(s32[32]{0:T(128)} %param.14) | copy-start | bytes 388
  65.5 20.1 %copy-start.3 = (f32[4096]{0:T(1024)S(1)}, f32[4096]{0:T(1024)}, u32[]{:S(2)}) copy-start(f32[4096]{0:T(1024)} %param.9) | copy-start | bytes 49156
  66.5 9.8 %collective-permute-start.3 = (bf16[256,512]{1,0:T(8,128)(2,1)S(1)}, bf16[256,512]{1,0:T(8,128)(2,1)S(1)}, u32[]{:S(2)}, u32[]{:S(2)}) collective-permute-start(bf16[256,512]{1,0:T(8,128)(2,1)S(1)} %slice.18), channel_id=1, source_target_pairs={{0,384},{8,392},{16,400},{24,408},{32,416},{40,424},{48,432},{56,4... | collective-permute-start | bytes 786440 | tf_op jit(solution)/shard_map/ppermute | solution.py:206
  76.3 9.3 %collective-permute-start.4 = (bf16[2048,512]{1,0:T(8,128)(2,1)S(1)}, bf16[2048,512]{1,0:T(8,128)(2,1)}, u32[]{:S(2)}, u32[]{:S(2)}) collective-permute-start(bf16[2048,512]{1,0:T(8,128)(2,1)S(1)} %constant_dynamic-update-slice_fusion), channel_id=1, source_target_pairs={{0,8},{8,0},{16,24},{24,16},{32,40},{40,32},{48,56},{56,48},{64,72... | collective-permute-start | bytes 6291464 | tf_op jit(solution)/shard_map/ppermute | solution.py:208
  78.3 12.6 %collective-permute-start.5 = (bf16[2048,512]{1,0:T(8,128)(2,1)}, bf16[2048,512]{1,0:T(8,128)(2,1)}, u32[]{:S(2)}, u32[]{:S(2)}) collective-permute-start(bf16[2048,512]{1,0:T(8,128)(2,1)} %ko_ref.1), channel_id=1, source_target_pairs={{0,8},{8,0},{16,24},{24,16},{32,40},{40,32},{48,56},{56,48},{64,72... | collective-permute-start | bytes 6291464 | tf_op jit(solution)/shard_map/ppermute | solution.py:199
  80.7 10.2 %collective-permute-start.6 = (bf16[2048,512]{1,0:T(8,128)(2,1)}, bf16[2048,512]{1,0:T(8,128)(2,1)}, u32[]{:S(2)}, u32[]{:S(2)}) collective-permute-start(bf16[2048,512]{1,0:T(8,128)(2,1)} %vo_ref.1), channel_id=1, source_target_pairs={{0,8},{8,0},{16,24},{24,16},{32,40},{40,32},{48,56},{56,48},{64,72... | collective-permute-start | bytes 6291464 | tf_op jit(solution)/shard_map/ppermute | solution.py:200
  85.6 1.6 copy-start.1
  110.2 6.4 %collective-permute-start.7 = (bf16[2048,512]{1,0:T(8,128)(2,1)}, bf16[2048,512]{1,0:T(8,128)(2,1)S(1)}, u32[]{:S(2)}, u32[]{:S(2)}) collective-permute-start(bf16[2048,512]{1,0:T(8,128)(2,1)} %bitcast.19), channel_id=1, source_target_pairs={{0,8},{8,0},{16,24},{24,16},{32,40},{40,32},{48,56},{56,48},{64,72... | collective-permute-start | bytes 6291464 | tf_op jit(solution)/shard_map/ppermute | solution.py:212
  150.6 1.6 copy-start
  152.2 1.6 copy-start.2
Sparse Core Ops, SparseCore 0:
  9.4 48.2 all-gather.7
  59.8 33.3 all-gather.5
  110.2 40.3 all-gather.9

commit v2 on v1

v2 whole, which is shorter than its diff:
```python
import functools

import jax
import jax.numpy as jnp
from jax import lax
from jax.experimental import pallas as pl
from jax.experimental.pallas import tpu as pltpu
from jax.sharding import PartitionSpec as P

DK = 64
NX, NZ = 4, 8
CUTS = (3, 1)


def place(x, z, core):
    return ((x % NX) * NZ + z % NZ) * 2 + core


PARTNERS = [(i, i ^ 1) for i in range(2 * NX * NZ)]
Z_GROUPS = [[place(x, z, core) for z in range(NZ)] for x in range(NX) for core in range(2)]
X_GROUPS = [[place(x, z, core) for x in range(NX)] for z in range(NZ) for core in range(2)]


def project_kernel(normalize, n_in, core_ref, *refs):
    x_refs, (gain_ref, own_ref, far_ref, o_ref, xs, w, sems) = refs[:n_in], refs[n_in:]
    blocks, rows, width = xs.shape
    core = core_ref[0]
    loads, at = [], 0
    for i, x_ref in enumerate(x_refs):
        there = slice(at, at + x_ref.shape[2])
        loads.append(pltpu.make_async_copy(x_ref, xs.at[:, :, there], sems.at[2 * NX + i]))
        at += x_ref.shape[2]
    own = [pltpu.make_async_copy(own_ref.at[i], w.at[i, :, core], sems.at[i]) for i in range(NX)]
    far = [
        pltpu.make_async_copy(far_ref.at[i], w.at[i, :, 1 - core], sems.at[NX + i])
        for i in range(NX)
    ]
    for copy in loads:
        copy.start()
    for i in range(NX):
        own[i].start()
        far[i].start()
    for copy in loads:
        copy.wait()
    if normalize:
        square = jnp.zeros((rows, width), jnp.float32)
        for b in range(blocks):
            part = xs[b].astype(jnp.float32)
            square = square + part * part
        mean = jnp.sum(square, axis=1, keepdims=True) / (blocks * width)
        scale = lax.rsqrt(mean + 1e-06)
        for b in range(blocks):
            part = xs[b].astype(jnp.float32)
            xs[b] = (part * scale * gain_ref[b]).astype(jnp.bfloat16)
    each = blocks // NX
    depth = NZ // each
    acc = jnp.zeros(o_ref.shape, jnp.float32)
    for i in range(NX):
        own[i].wait()
        far[i].wait()
        for j in range(each):
            part = w[i, j * depth : (j + 1) * depth].reshape(width, o_ref.shape[1])
            acc = acc + jnp.dot(xs[i * each + j], part, preferred_element_type=jnp.float32)
    o_ref[...] = acc.astype(jnp.bfloat16)


def project(normalize, core, xs, gain, own, far):
    blocks, rows = xs[0].shape[:2]
    width = sum(x.shape[2] for x in xs)
    piece, out = own.shape[-2:]
    anywhere = pl.BlockSpec(memory_space=pl.ANY)
    return pl.pallas_call(
        functools.partial(project_kernel, normalize, len(xs)),
        out_shape=jax.ShapeDtypeStruct((rows, out), jnp.bfloat16),
        grid_spec=pltpu.PrefetchScalarGridSpec(
            num_scalar_prefetch=1,
            grid=(1,),
            in_specs=[anywhere] * len(xs)
            + [pl.BlockSpec((blocks, 1, width), lambda i, s: (0, 0, 0)), anywhere, anywhere],
            out_specs=pl.BlockSpec((rows, out), lambda i, s: (0, 0)),
            scratch_shapes=[
                pltpu.VMEM((blocks, rows, width), jnp.bfloat16),
                pltpu.VMEM((NX, NZ, 2, piece, out), jnp.bfloat16),
                pltpu.SemaphoreType.DMA((2 * NX + len(xs),)),
            ],
        ),
        compiler_params=pltpu.CompilerParams(vmem_limit_bytes=60 << 20),
        cost_estimate=pl.CostEstimate(
            flops=2 * rows * blocks * width * out,
            bytes_accessed=2 * blocks * width * (rows + out),
            transcendentals=0,
        ),
        name="project",
    )(core, *xs, gain, own, far)


def attend_kernel(step, start, s_ref, q_ref, ko_ref, vo_ref, kf_ref, vf_ref, o_ref, keys, vals, sems):
    half = ko_ref.shape[0]
    rows = q_ref.shape[0]
    pair, tile = 2 * DK, 256
    turn, turns = pl.program_id(0), pl.num_programs(0)
    slot = lax.rem(turn, 2)

    def copies(h, into):
        lanes = pl.ds(pl.multiple_of((start + h) * pair, pair), pair)
        return [
            pltpu.make_async_copy(ko_ref.at[:, lanes], keys.at[into, :half], sems.at[into, 0]),
            pltpu.make_async_copy(kf_ref.at[:, lanes], keys.at[into, half:], sems.at[into, 1]),
            pltpu.make_async_copy(vo_ref.at[:, lanes], vals.at[into, :half, :pair], sems.at[into, 2]),
            pltpu.make_async_copy(vf_ref.at[:, lanes], vals.at[into, half:, :pair], sems.at[into, 3]),
        ]

    @pl.when(turn == 0)
    def _():
        for copy in copies(turn, slot):
            copy.start()
        for base, count in ((0, s_ref[0]), (half, s_ref[1])):
            for c in range(0, half, tile):
                valid = lax.broadcasted_iota(jnp.int32, (tile, pair), 0) + c < count
                ones = jnp.where(valid, 1.0, 0.0).astype(jnp.bfloat16)
                for into in range(2):
                    vals[into, base + c : base + c + tile, pair:] = ones

    @pl.when(turn + 1 < turns)
    def _():
        for copy in copies(turn + 1, 1 - slot):
            copy.start()

    for copy in copies(turn, slot):
        copy.wait()
    for base, count in ((0, s_ref[0]), (half, s_ref[1])):
        for c in range(0, half, tile):

            @pl.when(c + tile > count)
            def _():
                there = slice(base + c, base + c + tile)
                valid = lax.broadcasted_iota(jnp.int32, (tile, 1), 0) + c < count
                keys[slot, there] = jnp.where(valid, keys[slot, there], keys[slot, base : base + 1])
                v = vals[slot, there, :pair]
                vals[slot, there, :pair] = jnp.where(valid, v, jnp.zeros_like(v))
    first = lax.broadcasted_iota(jnp.int32, (1, pair), 1) < DK
    q = q_ref[...]
    zero = jnp.zeros_like(q)
    both = jnp.concatenate([jnp.where(first, q, zero), jnp.where(first, zero, q)], axis=0)
    top = acc = None
    for c in range(0, 2 * half, step):
        scores = lax.dot_general(both, keys[slot, c : c + step], (((1,), (1,)), ((), ())), preferred_element_type=jnp.float32)
        new_top = jnp.max(scores, axis=1, keepdims=True)
        if top is not None:
            new_top = jnp.maximum(top, new_top)
        weights = jnp.exp(scores - new_top).astype(jnp.bfloat16)
        part = jnp.dot(weights, vals[slot, c : c + step], preferred_element_type=jnp.float32)
        acc = part if top is None else acc * jnp.exp(top - new_top) + part
        top = new_top
    out = acc[:, :pair] / acc[:, pair:]
    live = lax.broadcasted_iota(jnp.int32, (rows, 1), 0) < s_ref[2]
    o_ref[...] = jnp.where(live, jnp.where(first, out[:rows], out[rows:]), 0.0).astype(jnp.bfloat16)


def attend(counts, q, own_k, own_v, far_k, far_v, start, pairs):
    rows = q.shape[0]
    width = pairs * 2 * DK
    half = own_k.shape[0]
    pair = 2 * DK
    hbm = pl.BlockSpec(memory_space=pl.ANY)
    qs = pl.BlockSpec((rows, pair), lambda h, s: (0, start + h))
    os = pl.BlockSpec((rows, pair), lambda h, s: (0, h))
    return pl.pallas_call(
        functools.partial(attend_kernel, 512, start),
        out_shape=jax.ShapeDtypeStruct((rows, width), jnp.bfloat16),
        grid_spec=pltpu.PrefetchScalarGridSpec(
            num_scalar_prefetch=1,
            grid=(pairs,),
            in_specs=[qs, hbm, hbm, hbm, hbm],
            out_specs=os,
            scratch_shapes=[
                pltpu.VMEM((2, 2 * half, pair), jnp.bfloat16),
                pltpu.VMEM((2, 2 * half, 2 * pair), jnp.bfloat16),
                pltpu.SemaphoreType.DMA((2, 4)),
            ],
        ),
        compiler_params=pltpu.CompilerParams(vmem_limit_bytes=60 << 20),
        cost_estimate=pl.CostEstimate(
            flops=16 * rows * width * half,
            bytes_accessed=8 * half * width,
            transcendentals=2 * rows * width // DK * half,
        ),
        name="attend",
    )(counts, q, own_k, own_v, far_k, far_v)


def local(dec_states, norm_gain, w_query, enc_keys, enc_values, w_out, tgt_lengths, src_lengths):
    heads = lax.axis_size("head")
    position = lax.axis_index("ctx")
    core = position % 2
    example = position // 2
    rows, width = dec_states.shape
    piece = w_query.shape[0]
    enc_count = enc_keys.shape[0]
    slot_ids = jnp.arange(tgt_lengths.shape[0], dtype=jnp.int32)
    tgt_len = jnp.sum(jnp.where(slot_ids == example, tgt_lengths, 0))
    src_len = jnp.sum(jnp.where(slot_ids == example, src_lengths, 0))
    counts = jnp.stack(
        [src_len - core * enc_count, src_len - (1 - core) * enc_count, tgt_len - core * rows]
    ).astype(jnp.int32)
    side = core.reshape(1).astype(jnp.int32)

    states = lax.all_gather(dec_states, "head")

    pieces = jnp.broadcast_to(
        jnp.concatenate([w_query, w_out], axis=1)[None], (NZ, piece, 2 * width)
    )
    pieces = lax.all_to_all(pieces, "ctx", 0, 0, axis_index_groups=Z_GROUPS)
    wq = pieces[:, :, :width]
    wo = pieces[:, :, width:]
    wo_own = lax.all_gather(wo, "ctx", axis_index_groups=X_GROUPS)

    wq = jnp.broadcast_to(wq[None], (NX, NZ, piece, width))
    wq_own = lax.all_to_all(wq, "ctx", 0, 0, axis_index_groups=X_GROUPS)
    wq_own, states = lax.optimization_barrier((wq_own, states))
    wq_far = lax.ppermute(wq_own, "ctx", PARTNERS)
    wq_own, keys, values = lax.optimization_barrier((wq_own, enc_keys, enc_values))
    far_keys = lax.ppermute(keys, "ctx", PARTNERS)
    far_values = lax.ppermute(values, "ctx", PARTNERS)
    wo_far = lax.ppermute(wo_own, "ctx", PARTNERS)

    gain = norm_gain.reshape(heads, 1, width)
    queries = project(True, side, [states], gain, wq_own, wq_far)
    gathered, start = [], 0
    for pairs in CUTS:
        attended = attend(
            counts, queries, enc_keys, enc_values, far_keys, far_values, start, pairs
        )
        gathered.append(lax.all_gather(attended, "head"))
        start += pairs
    return project(False, side, gathered, gain, wo_own, wo_far)


def solution(mesh):
    placed = (
        P("ctx", "head"),
        P(),
        P("ctx", "head"),
        P("ctx", "head"),
        P("ctx", "head"),
        P("ctx", "head"),
        P(),
        P(),
    )
    return jax.shard_map(
        local, mesh=mesh, in_specs=placed, out_specs=P("ctx", "head"), check_vma=False
    )
```

time: 164 us -> 160 us (0.976)
  blocking collectives: 38.8 us -> 69.7 us
  waiting for transfers between devices: 53 us -> 24.2 us
  starting transfers between devices: 20.4 us -> 13.6 us
  local copies, waits for them, and re-layouts: 8.17 us -> 3.34 us
  Pallas kernels: 25.9 us -> 29.8 us
    all_gather x2, waiting for transfers between devices: 34.1 us -> 0.66 us  [the longest x1 0.64 us: local(): gathered.append(lax.all_gather(attended, 'head'))]
    all_gather x0 -> x1, blocking collectives: none -> 30.8 us  [local(): gathered.append(lax.all_gather(attended, 'head'))]
    all_to_all x0 -> x1, waiting for transfers between devices: none -> 22.1 us  [local(): wq_own = lax.all_to_all(wq, 'ctx', 0, 0, axis_index_groups=X_GROUPS)]
    ppermute x8 -> x4, waiting for transfers between devices: 18.1 us -> 0.01 us  [the longest x1 0.01 us: local(): far_keys = lax.ppermute(keys, 'ctx', PARTNERS)]
    ppermute x8 -> x4, starting transfers between devices: 20.3 us -> 8.65 us  [the longest x1 2.41 us: local(): far_keys = lax.ppermute(keys, 'ctx', PARTNERS)]
    unnamed x16 -> x8, local copies, waits for them, and re-layouts: 5.97 us -> 0.69 us
    all_to_all x0 -> x1, starting transfers between devices: none -> 4.9 us  [local(): wq_own = lax.all_to_all(wq, 'ctx', 0, 0, axis_index_groups=X_GROUPS)]
    pallas_call x3 -> x4, Pallas kernels: 25.9 us -> 29.8 us  [the longest x2 19.4 us: attend(): pl.pallas_call(functools.partial(attend_kernel, 512, start), out_shape=ja...]
  transfers between devices with their start and end apart: 11 -> 8, of which waited for: 5 -> 2; matrix products, arithmetic and copies ran while one was open for 3% -> 3% of each run, Pallas kernels for 14% -> 16%
where the time goes in v2:
time: 160 us; the launch traced here: 158 us
  blocking collectives  69.7 us (44%)
  Pallas kernels  29.8 us (19%)
  waiting for transfers between devices  24.2 us (15%)
  between operations  15.1 us (9%)
  starting transfers between devices  13.6 us (8%)
  local copies, waits for them, and re-layouts  3.34 us (2%)
  other arithmetic  2.1 us (1%)
    all_to_all x1, blocking collectives, local(): pieces = lax.all_to_all(pieces, 'ctx', 0, 0, axis_index_groups=Z_GROUPS)  38.8 us
    all_gather x1, blocking collectives, local(): gathered.append(lax.all_gather(attended, 'head'))  30.8 us
    all_to_all x1, waiting for transfers between devices, local(): wq_own = lax.all_to_all(wq, 'ctx', 0, 0, axis_index_groups=X_GROUPS)  22.1 us
    pallas_call x2, Pallas kernels, attend(): pl.pallas_call(functools.partial(attend_kernel, 512, start), out_shape=ja...  19.4 us
    pallas_call x2, Pallas kernels, project(): pl.pallas_call(functools.partial(project_kernel, normalize, len(xs)), out...  10.4 us
    all_to_all x1, starting transfers between devices, local(): wq_own = lax.all_to_all(wq, 'ctx', 0, 0, axis_index_groups=X_GROUPS)  4.9 us
  transfers between devices with their start and end apart: 8, of which 2 were waited for; matrix products, arithmetic and copies ran while one was open for 3% of the time, Pallas kernels for 16%

profile of v2, /device:TPU:6, one launch (start us, length us, event | category | flops | bytes accessed | tf_op | source)
XLA Modules:
  0.0 157.9 jit_solution(15874882102522591450)
XLA Ops:
  6.5 0.7 all-gather.8.cloned.1.call-update
  7.3 0.9 pad_maximum_fusion
  8.1 0.1 broadcast_in_dim.18
  8.3 38.8 %all_to_all.10 = bf16[8,64,1024]{2,1,0:T(8,128)(2,1)S(1)} all-to-all(bf16[8,64,1024]{2,1,0:T(8,128)(2,1)S(1)} %broadcast_in_dim.18), channel_id=1, replica_groups={{0,16,32,48,64,80,96,112},{8,24,40,56,72,88,104,120},{128,144,160,176,1..., dimensions={0} | all-to-all | bytes 2097152 | tf_op jit(solution)/shard_map/all_to_all | solution.py:213
  47.1 1.0 fusion.2
  48.1 1.6 %broadcast_in_dim.19 = bf16[4,8,64,512]{3,2,1,0:T(8,128)(2,1)} broadcast(bf16[8,64,512]{2,1,0:T(8,128)(2,1)S(1)} %get-tuple-element.16), dimensions={1,2,3} | broadcast | bytes 2621440 | tf_op jit(solution)/shard_map/broadcast_in_dim | solution.py:218
  49.6 4.9 %all-to-all-start.1 = ((bf16[4,8,64,512]{3,2,1,0:T(8,128)(2,1)}), bf16[4,8,64,512]{3,2,1,0:T(8,128)(2,1)S(1)}, u32[]{:S(2)}, u32[]{:S(2)}) async-start(bf16[4,8,64,512]{3,2,1,0:T(8,128)(2,1)} %broadcast_in_dim.19), calls=%async_computation.1 | async-start | bytes 4194304 | tf_op jit(solution)/shard_map/all_to_all | solution.py:219
  54.6 0.7 all-gather.12.cloned.1.call-update
  55.3 0.0 all-gather.10.cloned.1.call-start
  55.3 22.1 %all-to-all-done.1.refs_2_ = bf16[4,8,64,512]{3,2,1,0:T(8,128)(2,1)S(1)} async-done(((bf16[4,8,64,512]{3,2,1,0:T(8,128)(2,1)}), bf16[4,8,64,512]{3,2,1,0:T(8,128)(2,1)S(1)}, u32[]{:S(2)}, u32[]{:S(2)}) %all-to-all-start.1) | async-done | bytes 2097184 | tf_op jit(solution)/shard_map/all_to_all | solution.py:219
  77.4 1.9 %collective-permute-start = (bf16[4,8,64,512]{3,2,1,0:T(8,128)(2,1)S(1)}, bf16[4,8,64,512]{3,2,1,0:T(8,128)(2,1)}, u32[]{:S(2)}, u32[]{:S(2)}) collective-permute-start(bf16[4,8,64,512]{3,2,1,0:T(8,128)(2,1)S(1)} %all-to-all-done.1.refs_2_), channel_id=1, source_target_pairs={{0,8},{8,0},{16,24},{24,16},{32,40},{40,32},{48,56},{56,48},{64,72... | collective-permute-start | bytes 6291464 | tf_op jit(solution)/shard_map/ppermute | solution.py:221
  79.4 2.4 %collective-permute-start.1 = (bf16[2048,512]{1,0:T(8,128)(2,1)}, bf16[2048,512]{1,0:T(8,128)(2,1)}, u32[]{:S(2)}, u32[]{:S(2)}) collective-permute-start(bf16[2048,512]{1,0:T(8,128)(2,1)} %ko_ref.3), channel_id=1, source_target_pairs={{0,8},{8,0},{16,24},{24,16},{32,40},{40,32},{48,56},{56,48},{64,72... | collective-permute-start | bytes 6291464 | tf_op jit(solution)/shard_map/ppermute | solution.py:223
  81.8 1.9 %collective-permute-start.2 = (bf16[2048,512]{1,0:T(8,128)(2,1)}, bf16[2048,512]{1,0:T(8,128)(2,1)}, u32[]{:S(2)}, u32[]{:S(2)}) collective-permute-start(bf16[2048,512]{1,0:T(8,128)(2,1)} %vo_ref.3), channel_id=1, source_target_pairs={{0,8},{8,0},{16,24},{24,16},{32,40},{40,32},{48,56},{56,48},{64,72... | collective-permute-start | bytes 6291464 | tf_op jit(solution)/shard_map/ppermute | solution.py:224
  83.8 0.6 fusion
  86.2 0.6 pad_add_fusion.s_ref
  86.8 5.7 %project.2.q_ref = bf16[256,512]{1,0:T(8,128)(2,1)} custom-call(s32[1]{0:T(128)} %bitcast.core_ref, bf16[8,256,512]{2,1,0:T(8,128)(2,1)} %bitcast.11, f32[8,1,512]{2,1,0:T(1,128)} %bitcast.14, bf16[4,8,64,512]{3,2,1,0:T(8,128)(2,1)} %copy-done, bf16[4,8,64,512]{3,2,1,0:T(8,128)(2,1)} %collective-permute-done.refs_3_), custom_call_target="tpu_custom_call" | custom-call | flops 1073741824 | bytes 6291456 | tf_op jit(solution)/shard_map/project/pallas_call | solution.py:72
  92.5 12.8 %attend.2 = bf16[256,384]{1,0:T(8,128)(2,1)} custom-call(s32[3]{0:T(128)} %pad_add_fusion.s_ref, bf16[256,512]{1,0:T(8,128)(2,1)} %project.2.q_ref, bf16[2048,512]{1,0:T(8,128)(2,1)} %ko_ref.3, bf16[2048,512]{1,0:T(8,128)(2,1)} %vo_ref.3, bf16[2048,512]{1,0:T(8,128)(2,1)} %collective-permute-done.1.kf_ref, bf16[2048,512]{1,0:T(8,128)(2,1)} %collective-permute-done.2.vf_ref), custom_call_target="tpu_custom_call" | custom-call | flops 3221225472 | bytes 6291456 | tf_op jit(solution)/shard_map/attend/pallas_call | solution.py:168
  105.3 0.0 all-gather.12.cloned.1.call-done
  105.4 2.4 %collective-permute-start.3 = (bf16[4,8,64,512]{3,2,1,0:T(8,128)(2,1)}, bf16[4,8,64,512]{3,2,1,0:T(8,128)(2,1)S(1)}, u32[]{:S(2)}, u32[]{:S(2)}) collective-permute-start(bf16[4,8,64,512]{3,2,1,0:T(8,128)(2,1)} %bitcast.9), channel_id=1, source_target_pairs={{0,8},{8,0},{16,24},{24,16},{32,40},{40,32},{48,56},{56,48},{64,72... | collective-permute-start | bytes 6291464 | tf_op jit(solution)/shard_map/ppermute | solution.py:225
  107.8 6.7 %attend.3 = bf16[256,128]{1,0:T(8,128)(2,1)} custom-call(s32[3]{0:T(128)} %pad_add_fusion.s_ref, bf16[256,512]{1,0:T(8,128)(2,1)} %project.2.q_ref, bf16[2048,512]{1,0:T(8,128)(2,1)} %ko_ref.3, bf16[2048,512]{1,0:T(8,128)(2,1)} %vo_ref.3, bf16[2048,512]{1,0:T(8,128)(2,1)} %collective-permute-done.1.kf_ref, bf16[2048,512]{1,0:T(8,128)(2,1)} %collective-permute-done.2.vf_ref), custom_call_target="tpu_custom_call" | custom-call | flops 1073741824 | bytes 2097152 | tf_op jit(solution)/shard_map/attend/pallas_call | solution.py:168
  114.4 30.8 %all-gather.2 = bf16[2048,128]{1,0:T(8,128)(2,1)} all-gather(bf16[256,128]{1,0:T(8,128)(2,1)} %attend.3), channel_id=4, replica_groups=mesh['ctx'=64,'head'=8] {'head'}, dimensions={0}, use_global_device_ids=true | all-gather | bytes 589824 | tf_op jit(solution)/shard_map/all_gather | solution.py:234
  145.3 0.6 all-gather.10.cloned.1.call-done
  145.9 0.7 copy-done.1
  146.6 4.7 %project.3 = bf16[256,512]{1,0:T(8,128)(2,1)} custom-call(s32[1]{0:T(128)} %bitcast.core_ref, bf16[8,256,384]{2,1,0:T(8,128)(2,1)} %bitcast.13, bf16[8,256,128]{2,1,0:T(8,128)(2,1)} %bitcast.12, f32[8,1,512]{2,1,0:T(1,128)} %bitcast.15, bf16[4,8,64,512]{3,2,1,0:T(8,128)(2,1)} %bitcast.10, bf16[4,8,64,512]{3,2,1,0:T(8,128)(2,1)} %copy-done.1), custom_call_target="tpu_custom_call" | custom-call | flops 1073741824 | bytes 6291456 | tf_op jit(solution)/shard_map/project/pallas_call | solution.py:72
  (15 shorter events, 0.0 us)
Async XLA Ops:
  6.5 70.9 %all-gather.8.cloned.1.call-start = ((), (), s32[]{:S(2)}) async-start(), calls=%async_computation.2 | async-start | bytes 2359296 | tf_op jit(solution)/shard_map/all_gather | solution.py:208
  49.6 34.1 %copy-start.2 = (s32[32]{0:T(128)S(1)}, s32[32]{0:T(128)}, u32[]{:S(2)}) copy-start(s32[32]{0:T(128)} %param.15) | copy-start | bytes 388
  49.6 34.1 %copy-start.3 = (s32[32]{0:T(128)S(1)}, s32[32]{0:T(128)}, u32[]{:S(2)}) copy-start(s32[32]{0:T(128)} %param.14) | copy-start | bytes 388
  49.6 27.8 %all-to-all-start.1 = ((bf16[4,8,64,512]{3,2,1,0:T(8,128)(2,1)}), bf16[4,8,64,512]{3,2,1,0:T(8,128)(2,1)S(1)}, u32[]{:S(2)}, u32[]{:S(2)}) async-start(bf16[4,8,64,512]{3,2,1,0:T(8,128)(2,1)} %broadcast_in_dim.19), calls=%async_computation.1 | async-start | bytes 4194304 | tf_op jit(solution)/shard_map/all_to_all | solution.py:219
  54.6 50.8 %all-gather.12.cloned.1.call-start = ((), (), s32[]{:S(2)}) async-start(), calls=%async_computation.4 | async-start | bytes 2621440 | tf_op jit(solution)/shard_map/all_gather | solution.py:216
  55.3 90.6 %all-gather.10.cloned.1.call-start = ((), (), s32[]{:S(2)}) async-start(), calls=%async_computation.3 | async-start | bytes 1769472 | tf_op jit(solution)/shard_map/all_gather | solution.py:234
  77.4 9.4 %copy-start = (bf16[4,8,64,512]{3,2,1,0:T(8,128)(2,1)}, bf16[4,8,64,512]{3,2,1,0:T(8,128)(2,1)S(1)}, u32[]{:S(2)}) copy-start(bf16[4,8,64,512]{3,2,1,0:T(8,128)(2,1)S(1)} %all-to-all-done.1.refs_2_) | copy-start | bytes 6291460
  77.4 9.4 %collective-permute-start = (bf16[4,8,64,512]{3,2,1,0:T(8,128)(2,1)S(1)}, bf16[4,8,64,512]{3,2,1,0:T(8,128)(2,1)}, u32[]{:S(2)}, u32[]{:S(2)}) collective-permute-start(bf16[4,8,64,512]{3,2,1,0:T(8,128)(2,1)S(1)} %all-to-all-done.1.refs_2_), channel_id=1, source_target_pairs={{0,8},{8,0},{16,24},{24,16},{32,40},{40,32},{48,56},{56,48},{64,72... | collective-permute-start | bytes 6291464 | tf_op jit(solution)/shard_map/ppermute | solution.py:221
  79.4 13.2 %collective-permute-start.1 = (bf16[2048,512]{1,0:T(8,128)(2,1)}, bf16[2048,512]{1,0:T(8,128)(2,1)}, u32[]{:S(2)}, u32[]{:S(2)}) collective-permute-start(bf16[2048,512]{1,0:T(8,128)(2,1)} %ko_ref.3), channel_id=1, source_target_pairs={{0,8},{8,0},{16,24},{24,16},{32,40},{40,32},{48,56},{56,48},{64,72... | collective-permute-start | bytes 6291464 | tf_op jit(solution)/shard_map/ppermute | solution.py:223
  81.8 10.7 %collective-permute-start.2 = (bf16[2048,512]{1,0:T(8,128)(2,1)}, bf16[2048,512]{1,0:T(8,128)(2,1)}, u32[]{:S(2)}, u32[]{:S(2)}) collective-permute-start(bf16[2048,512]{1,0:T(8,128)(2,1)} %vo_ref.3), channel_id=1, source_target_pairs={{0,8},{8,0},{16,24},{24,16},{32,40},{40,32},{48,56},{56,48},{64,72... | collective-permute-start | bytes 6291464 | tf_op jit(solution)/shard_map/ppermute | solution.py:224
  105.4 39.9 %collective-permute-start.3 = (bf16[4,8,64,512]{3,2,1,0:T(8,128)(2,1)}, bf16[4,8,64,512]{3,2,1,0:T(8,128)(2,1)S(1)}, u32[]{:S(2)}, u32[]{:S(2)}) collective-permute-start(bf16[4,8,64,512]{3,2,1,0:T(8,128)(2,1)} %bitcast.9), channel_id=1, source_target_pairs={{0,8},{8,0},{16,24},{24,16},{32,40},{40,32},{48,56},{56,48},{64,72... | collective-permute-start | bytes 6291464 | tf_op jit(solution)/shard_map/ppermute | solution.py:225
  145.3 1.3 copy-start.1
Sparse Core Ops, SparseCore 0:
  9.4 48.2 all-gather.7
  59.8 34.4 all-gather.11
  105.4 40.4 all-gather.9

commit v3 on v2

--- a/solution.py
+++ b/solution.py
@@ -21,77 +21,168 @@
 X_GROUPS = [[place(x, z, core) for x in range(NX)] for z in range(NZ) for core in range(2)]
 
 
-def project_kernel(normalize, n_in, core_ref, *refs):
-    x_refs, (gain_ref, own_ref, far_ref, o_ref, xs, w, sems) = refs[:n_in], refs[n_in:]
-    blocks, rows, width = xs.shape
-    core = core_ref[0]
-    loads, at = [], 0
-    for i, x_ref in enumerate(x_refs):
-        there = slice(at, at + x_ref.shape[2])
-        loads.append(pltpu.make_async_copy(x_ref, xs.at[:, :, there], sems.at[2 * NX + i]))
-        at += x_ref.shape[2]
-    own = [pltpu.make_async_copy(own_ref.at[i], w.at[i, :, core], sems.at[i]) for i in range(NX)]
-    far = [
-        pltpu.make_async_copy(far_ref.at[i], w.at[i, :, 1 - core], sems.at[NX + i])
-        for i in range(NX)
-    ]
-    for copy in loads:
-        copy.start()
-    for i in range(NX):
-        own[i].start()
-        far[i].start()
-    for copy in loads:
-        copy.wait()
-    if normalize:
-        square = jnp.zeros((rows, width), jnp.float32)
-        for b in range(blocks):
-            part = xs[b].astype(jnp.float32)
-            square = square + part * part
-        mean = jnp.sum(square, axis=1, keepdims=True) / (blocks * width)
-        scale = lax.rsqrt(mean + 1e-06)
-        for b in range(blocks):
-            part = xs[b].astype(jnp.float32)
-            xs[b] = (part * scale * gain_ref[b]).astype(jnp.bfloat16)
+def normalize_kernel(x_ref, gain_ref, o_ref):
+    blocks, rows, width = x_ref.shape
+    square = jnp.zeros((rows, width), jnp.float32)
+    for b in range(blocks):
+        part = x_ref[b].astype(jnp.float32)
+        square = square + part * part
+    mean = jnp.sum(square, axis=1, keepdims=True) / (blocks * width)
+    scale = lax.rsqrt(mean + 1e-06)
+    first = lax.broadcasted_iota(jnp.int32, (1, 2 * DK), 1) < DK
+    for b in range(blocks):
+        part = x_ref[b].astype(jnp.float32) * scale * gain_ref[b]
+        for j in range(width // (4 * DK)):
+            one = part[:, 4 * DK * j : 4 * DK * j + 2 * DK]
+            two = part[:, 4 * DK * j + 2 * DK : 4 * DK * (j + 1)]
+            lanes = slice(2 * DK * j, 2 * DK * (j + 1))
+            even = jnp.where(first, one, pltpu.roll(two, DK, 1))
+            odd = jnp.where(first, pltpu.roll(one, DK, 1), two)
+            o_ref[0, b, :, lanes] = even.astype(jnp.bfloat16)
+            o_ref[1, b, :, lanes] = odd.astype(jnp.bfloat16)
+
+
+def normalize(x, gain):
+    blocks, rows, width = x.shape
+    tile = 64
+    return pl.pallas_call(
+        normalize_kernel,
+        out_shape=jax.ShapeDtypeStruct((2, blocks, rows, width // 2), jnp.bfloat16),
+        grid=(rows // tile,),
+        in_specs=[
+            pl.BlockSpec((blocks, tile, width), lambda i: (0, i, 0)),
+            pl.BlockSpec((blocks, 1, width), lambda i: (0, 0, 0)),
+        ],
+        out_specs=pl.BlockSpec((2, blocks, tile, width // 2), lambda i: (0, 0, i, 0)),
+        compiler_params=pltpu.CompilerParams(vmem_limit_bytes=58 << 20),
+        cost_estimate=pl.CostEstimate(
+            flops=8 * rows * blocks * width,
+            bytes_accessed=4 * blocks * width * rows,
+            transcendentals=rows,
+        ),
+        name="normalize",
+    )(x, gain)
+
+
+def query_kernel(side_ref, x_ref, w_ref, *refs):
+    sum_ref = refs[0] if len(refs) == 5 else None
+    o_ref, xs, w, sems = refs[-4:]
+    blocks = xs.shape[0]
+    each = blocks // NX
+    x_copies, w_copies = [], []
+    for i in range(NX):
+        there = slice(i * each, (i + 1) * each)
+        x_copies.append(
+            pltpu.make_async_copy(x_ref.at[side_ref[0], there], xs.at[there], sems.at[0, i])
+        )
+        w_copies.append(pltpu.make_async_copy(w_ref.at[i], w.at[i], sems.at[1, i]))
+    for i in range(NX):
+        x_copies[i].start()
+        w_copies[i].start()
+    depth = NZ // each
+    total = jnp.zeros(o_ref.shape, jnp.float32) if sum_ref is None else sum_ref[...]
+    for i in range(NX):
+        x_copies[i].wait()
+        w_copies[i].wait()
+        for j in range(each):
+            part = w[i, j * depth : (j + 1) * depth].reshape(xs.shape[2], o_ref.shape[1])
+            total = total + jnp.dot(xs[i * each + j], part, preferred_element_type=jnp.float32)
+    o_ref[...] = total.astype(o_ref.dtype)
+
+
+def query_part(side, x, weights, partial=None):
+    _, blocks, rows, half = x.shape
+    piece, out = weights.shape[2:]
+    whole = pl.BlockSpec((rows, out), lambda i, s: (0, 0))
+    anywhere = pl.BlockSpec(memory_space=pl.ANY)
+    more = [] if partial is None else [partial]
+    return pl.pallas_call(
+        query_kernel,
+        out_shape=jax.ShapeDtypeStruct(
+            (rows, out), jnp.float32 if partial is None else jnp.bfloat16
+        ),
+        grid_spec=pltpu.PrefetchScalarGridSpec(
+            num_scalar_prefetch=1,
+            grid=(1,),
+            in_specs=[anywhere, anywhere] + [whole] * len(more),
+            out_specs=whole,
+            scratch_shapes=[
+                pltpu.VMEM((blocks, rows, half), jnp.bfloat16),
+                pltpu.VMEM((NX, NZ, piece, out), jnp.bfloat16),
+                pltpu.SemaphoreType.DMA((2, NX)),
+            ],
+        ),
+        compiler_params=pltpu.CompilerParams(vmem_limit_bytes=24 << 20),
+        cost_estimate=pl.CostEstimate(
+            flops=2 * rows * blocks * half * out,
+            bytes_accessed=2 * blocks * half * (rows + out),
+            transcendentals=0,
+        ),
+        name="query_part",
+    )(side, x, weights, *more)
+
+
+def output_kernel(n_in, side_ref, *refs):
+    x_refs, (own_ref, far_ref, o_ref, xs, w, sems) = refs[:n_in], refs[n_in:]
+    blocks, _, width = xs.shape
+    core = side_ref[0]
     each = blocks // NX
     depth = NZ // each
+    copies = []
+    for i in range(NX):
+        blocks_of = slice(i * each, (i + 1) * each)
+        group, at = [], 0
+        for k, x_ref in enumerate(x_refs):
+            lanes = slice(at, at + x_ref.shape[2])
+            group.append(
+                pltpu.make_async_copy(x_ref.at[blocks_of], xs.at[blocks_of, :, lanes], sems.at[i, k])
+            )
+            at += x_ref.shape[2]
+        group.append(pltpu.make_async_copy(own_ref.at[i], w.at[i, :, core], sems.at[i, n_in]))
+        group.append(
+            pltpu.make_async_copy(far_ref.at[i], w.at[i, :, 1 - core], sems.at[i, n_in + 1])
+        )
+        copies.append(group)
+    for group in copies:
+        for copy in group:
+            copy.start()
     acc = jnp.zeros(o_ref.shape, jnp.float32)
     for i in range(NX):
-        own[i].wait()
-        far[i].wait()
+        for copy in copies[i]:
+            copy.wait()
         for j in range(each):
             part = w[i, j * depth : (j + 1) * depth].reshape(width, o_ref.shape[1])
             acc = acc + jnp.dot(xs[i * each + j], part, preferred_element_type=jnp.float32)
     o_ref[...] = acc.astype(jnp.bfloat16)
 
 
-def project(normalize, core, xs, gain, own, far):
+def output_product(side, xs, own, far):
     blocks, rows = xs[0].shape[:2]
     width = sum(x.shape[2] for x in xs)
-    piece, out = own.shape[-2:]
+    piece, out = own.shape[2:]
     anywhere = pl.BlockSpec(memory_space=pl.ANY)
     return pl.pallas_call(
-        functools.partial(project_kernel, normalize, len(xs)),
+        functools.partial(output_kernel, len(xs)),
         out_shape=jax.ShapeDtypeStruct((rows, out), jnp.bfloat16),
         grid_spec=pltpu.PrefetchScalarGridSpec(
             num_scalar_prefetch=1,
             grid=(1,),
-            in_specs=[anywhere] * len(xs)
-            + [pl.BlockSpec((blocks, 1, width), lambda i, s: (0, 0, 0)), anywhere, anywhere],
+            in_specs=[anywhere] * (len(xs) + 2),
             out_specs=pl.BlockSpec((rows, out), lambda i, s: (0, 0)),
             scratch_shapes=[
                 pltpu.VMEM((blocks, rows, width), jnp.bfloat16),
                 pltpu.VMEM((NX, NZ, 2, piece, out), jnp.bfloat16),
-                pltpu.SemaphoreType.DMA((2 * NX + len(xs),)),
+                pltpu.SemaphoreType.DMA((NX, len(xs) + 2)),
             ],
         ),
-        compiler_params=pltpu.CompilerParams(vmem_limit_bytes=60 << 20),
+        compiler_params=pltpu.CompilerParams(vmem_limit_bytes=56 << 20),
         cost_estimate=pl.CostEstimate(
             flops=2 * rows * blocks * width * out,
             bytes_accessed=2 * blocks * width * (rows + out),
             transcendentals=0,
         ),
-        name="project",
-    )(core, *xs, gain, own, far)
+        name="output_product",
+    )(side, *xs, own, far)
 
 
 def attend_kernel(step, start, s_ref, q_ref, ko_ref, vo_ref, kf_ref, vf_ref, o_ref, keys, vals, sems):
@@ -126,9 +217,9 @@
         for copy in copies(turn + 1, 1 - slot):
             copy.start()
 
-    for copy in copies(turn, slot):
-        copy.wait()
-    for base, count in ((0, s_ref[0]), (half, s_ref[1])):
+    def arrive(k, base, count):
+        for copy in (copies(turn, slot)[k], copies(turn, slot)[k + 2]):
+            copy.wait()
         for c in range(0, half, tile):
 
             @pl.when(c + tile > count)
@@ -138,12 +229,17 @@
                 keys[slot, there] = jnp.where(valid, keys[slot, there], keys[slot, base : base + 1])
                 v = vals[slot, there, :pair]
                 vals[slot, there, :pair] = jnp.where(valid, v, jnp.zeros_like(v))
+
     first = lax.broadcasted_iota(jnp.int32, (1, pair), 1) < DK
     q = q_ref[...]
     zero = jnp.zeros_like(q)
     both = jnp.concatenate([jnp.where(first, q, zero), jnp.where(first, zero, q)], axis=0)
     top = acc = None
     for c in range(0, 2 * half, step):
+        if c == 0:
+            arrive(0, 0, s_ref[0])
+        if c == half:
+            arrive(1, half, s_ref[1])
         scores = lax.dot_general(both, keys[slot, c : c + step], (((1,), (1,)), ((), ())), preferred_element_type=jnp.float32)
         new_top = jnp.max(scores, axis=1, keepdims=True)
         if top is not None:
@@ -179,7 +275,7 @@
                 pltpu.SemaphoreType.DMA((2, 4)),
             ],
         ),
-        compiler_params=pltpu.CompilerParams(vmem_limit_bytes=60 << 20),
+        compiler_params=pltpu.CompilerParams(vmem_limit_bytes=58 << 20),
         cost_estimate=pl.CostEstimate(
             flops=16 * rows * width * half,
             bytes_accessed=8 * half * width,
@@ -203,9 +299,12 @@
     counts = jnp.stack(
         [src_len - core * enc_count, src_len - (1 - core) * enc_count, tgt_len - core * rows]
     ).astype(jnp.int32)
-    side = core.reshape(1).astype(jnp.int32)
+    own_side = core.reshape(1).astype(jnp.int32)
+    far_side = 1 - own_side
 
     states = lax.all_gather(dec_states, "head")
+    far_keys = lax.ppermute(enc_keys, "ctx", PARTNERS)
+    far_values = lax.ppermute(enc_values, "ctx", PARTNERS)
 
     pieces = jnp.broadcast_to(
         jnp.concatenate([w_query, w_out], axis=1)[None], (NZ, piece, 2 * width)
@@ -215,17 +314,18 @@
     wo = pieces[:, :, width:]
     wo_own = lax.all_gather(wo, "ctx", axis_index_groups=X_GROUPS)
 
-    wq = jnp.broadcast_to(wq[None], (NX, NZ, piece, width))
-    wq_own = lax.all_to_all(wq, "ctx", 0, 0, axis_index_groups=X_GROUPS)
-    wq_own, states = lax.optimization_barrier((wq_own, states))
+    wq_own = lax.all_to_all(
+        jnp.broadcast_to(wq[None], (NX, NZ, piece, width)), "ctx", 0, 0, axis_index_groups=X_GROUPS
+    )
+    normed = normalize(states, norm_gain.reshape(heads, 1, width))
+    wq_own, normed, far_keys, far_values, counts, own_side, far_side = lax.optimization_barrier(
+        (wq_own, normed, far_keys, far_values, counts, own_side, far_side)
+    )
     wq_far = lax.ppermute(wq_own, "ctx", PARTNERS)
-    wq_own, keys, values = lax.optimization_barrier((wq_own, enc_keys, enc_values))
-    far_keys = lax.ppermute(keys, "ctx", PARTNERS)
-    far_values = lax.ppermute(values, "ctx", PARTNERS)
     wo_far = lax.ppermute(wo_own, "ctx", PARTNERS)
 
-    gain = norm_gain.reshape(heads, 1, width)
-    queries = project(True, side, [states], gain, wq_own, wq_far)
+    queries = query_part(own_side, normed, wq_own)
+    queries = query_part(far_side, normed, wq_far, queries)
     gathered, start = [], 0
     for pairs in CUTS:
         attended = attend(
@@ -233,7 +333,7 @@
         )
         gathered.append(lax.all_gather(attended, "head"))
         start += pairs
-    return project(False, side, gathered, gain, wo_own, wo_far)
+    return output_product(own_side, gathered, wo_own, wo_far)
 
 
 def solution(mesh):

time: 160 us -> 161 us (level)
  blocking collectives: 69.7 us -> 30.1 us
  waiting for transfers between devices: 24.2 us -> 47.6 us
  starting transfers between devices: 13.6 us -> 23.5 us
  local copies, waits for them, and re-layouts: 3.34 us -> 7.28 us
  Pallas kernels: 29.8 us -> 32.4 us
    all_to_all x1 -> x0, blocking collectives: 38.8 us -> none  [local(): pieces = lax.all_to_all(pieces, 'ctx', 0, 0, axis_index_groups=Z_GROUPS)]
    all_to_all x1 -> x2, waiting for transfers between devices: 22.1 us -> 44.7 us  [the longest x1 24.4 us: local(): pieces = lax.all_to_all(pieces, 'ctx', 0, 0, axis_index_groups=Z_GROUPS)]
    all_to_all x1 -> x2, starting transfers between devices: 4.9 us -> 15.2 us  [the longest x1 10.3 us: local(): pieces = lax.all_to_all(pieces, 'ctx', 0, 0, axis_index_groups=Z_GROUPS)]
    unnamed x8 -> x10, local copies, waits for them, and re-layouts: 0.69 us -> 3.61 us
    pallas_call x2, Pallas kernels: 19.4 us -> 21.4 us  [attend(): pl.pallas_call(functools.partial(attend_kernel, 512, start), out_shape=ja...]
    pallas_call x2 -> x4, Pallas kernels: 10.4 us -> 11 us  [the longest x1 4.62 us: normalize(): pl.pallas_call(normalize_kernel, out_shape=jax.ShapeDtypeStruct((2, block...]
  transfers between devices with their start and end apart: 8 -> 9, of which waited for: 2 -> 3; matrix products, arithmetic and copies ran while one was open for 3% -> 4% of each run, Pallas kernels for 16% -> 18%
where the time goes in v3:
time: 161 us; the launch traced here: 158 us
  waiting for transfers between devices  47.6 us (30%)
  Pallas kernels  32.4 us (20%)
  blocking collectives  30.1 us (19%)
  starting transfers between devices  23.5 us (15%)
  between operations  15.2 us (9%)
  local copies, waits for them, and re-layouts  7.28 us (5%)
  other arithmetic  2.16 us (1%)
    all_gather x1, blocking collectives, local(): gathered.append(lax.all_gather(attended, 'head'))  30.1 us
    all_to_all x1, waiting for transfers between devices, local(): pieces = lax.all_to_all(pieces, 'ctx', 0, 0, axis_index_groups=Z_GROUPS)  24.4 us
    pallas_call x2, Pallas kernels, attend(): pl.pallas_call(functools.partial(attend_kernel, 512, start), out_shape=ja...  21.4 us
    all_to_all x1, waiting for transfers between devices, local(): lax.all_to_all(jnp.broadcast_to(wq[None], (NX, NZ, piece, width)), 'ctx',...  20.3 us
    all_to_all x1, starting transfers between devices, local(): pieces = lax.all_to_all(pieces, 'ctx', 0, 0, axis_index_groups=Z_GROUPS)  10.3 us
    all_to_all x1, starting transfers between devices, local(): lax.all_to_all(jnp.broadcast_to(wq[None], (NX, NZ, piece, width)), 'ctx',...  4.9 us
    pallas_call x1, Pallas kernels, normalize(): pl.pallas_call(normalize_kernel, out_shape=jax.ShapeDtypeStruct((2, block...  4.62 us
    pallas_call x1, Pallas kernels, output_product(): pl.pallas_call(functools.partial(output_kernel, len(xs)), out_shape=jax.S...  4.07 us
  transfers between devices with their start and end apart: 9, of which 3 were waited for; matrix products, arithmetic and copies ran while one was open for 4% of the time, Pallas kernels for 18%

profile of v3, /device:TPU:6, one launch (start us, length us, event | category | flops | bytes accessed | tf_op | source)
XLA Modules:
  0.0 158.3 jit_solution(3930297813540089245)
XLA Ops:
  6.5 0.7 all-gather.8.cloned.1.call-update
  7.3 0.9 pad_maximum_fusion
  8.1 1.1 broadcast_in_dim.9
  9.3 10.3 %all-to-all-start = ((bf16[8,64,1024]{2,1,0:T(8,128)(2,1)}), bf16[8,64,1024]{2,1,0:T(8,128)(2,1)S(1)}, u32[]{:S(2)}, u32[]{:S(2)}) async-start(bf16[8,64,1024]{2,1,0:T(8,128)(2,1)} %broadcast_in_dim.9), calls=%async_computation | async-start | bytes 2097152 | tf_op jit(solution)/shard_map/all_to_all | solution.py:312
  19.6 1.9 %collective-permute-start = (bf16[2048,512]{1,0:T(8,128)(2,1)}, bf16[2048,512]{1,0:T(8,128)(2,1)}, u32[]{:S(2)}, u32[]{:S(2)}) collective-permute-start(bf16[2048,512]{1,0:T(8,128)(2,1)} %ko_ref.3), channel_id=1, source_target_pairs={{0,8},{8,0},{16,24},{24,16},{32,40},{40,32},{48,56},{56,48},{64,72... | collective-permute-start | bytes 6291464 | tf_op jit(solution)/shard_map/ppermute | solution.py:306
  21.5 2.4 %collective-permute-start.1 = (bf16[2048,512]{1,0:T(8,128)(2,1)}, bf16[2048,512]{1,0:T(8,128)(2,1)}, u32[]{:S(2)}, u32[]{:S(2)}) collective-permute-start(bf16[2048,512]{1,0:T(8,128)(2,1)} %vo_ref.3), channel_id=1, source_target_pairs={{0,8},{8,0},{16,24},{24,16},{32,40},{40,32},{48,56},{56,48},{64,72... | collective-permute-start | bytes 6291464 | tf_op jit(solution)/shard_map/ppermute | solution.py:307
  23.9 24.4 %all-to-all-done = bf16[8,64,1024]{2,1,0:T(8,128)(2,1)S(1)} async-done(((bf16[8,64,1024]{2,1,0:T(8,128)(2,1)}), bf16[8,64,1024]{2,1,0:T(8,128)(2,1)S(1)}, u32[]{:S(2)}, u32[]{:S(2)}) %all-to-all-start) | async-done | bytes 1048608 | tf_op jit(solution)/shard_map/all_to_all | solution.py:312
  48.3 0.9 fusion.2
  49.2 1.6 %broadcast_in_dim.18 = bf16[4,8,64,512]{3,2,1,0:T(8,128)(2,1)} broadcast(bf16[8,64,512]{2,1,0:T(8,128)(2,1)S(1)} %get-tuple-element.20), dimensions={1,2,3} | broadcast | bytes 2621440 | tf_op jit(solution)/shard_map/broadcast_in_dim | solution.py:318
  50.9 4.9 %all-to-all-start.1 = ((bf16[4,8,64,512]{3,2,1,0:T(8,128)(2,1)}), bf16[4,8,64,512]{3,2,1,0:T(8,128)(2,1)S(1)}, u32[]{:S(2)}, u32[]{:S(2)}) async-start(bf16[4,8,64,512]{3,2,1,0:T(8,128)(2,1)} %broadcast_in_dim.18), calls=%async_computation.1 | async-start | bytes 4194304 | tf_op jit(solution)/shard_map/all_to_all | solution.py:317
  55.8 0.7 all-gather.12.cloned.1.call-update
  59.8 4.6 %normalize.1.x_ref = bf16[2,8,256,256]{3,2,1,0:T(8,128)(2,1)} custom-call(bf16[8,256,512]{2,1,0:T(8,128)(2,1)} %bitcast.11, f32[8,1,512]{2,1,0:T(1,128)} %bitcast.14), custom_call_target="tpu_custom_call" | custom-call | flops 8388608 | bytes 4194304 | tf_op jit(solution)/shard_map/normalize/pallas_call | solution.py:48
  64.4 20.3 %all-to-all-done.1.w_ref = bf16[4,8,64,512]{3,2,1,0:T(8,128)(2,1)S(1)} async-done(((bf16[4,8,64,512]{3,2,1,0:T(8,128)(2,1)}), bf16[4,8,64,512]{3,2,1,0:T(8,128)(2,1)S(1)}, u32[]{:S(2)}, u32[]{:S(2)}) %all-to-all-start.1) | async-done | bytes 2097184 | tf_op jit(solution)/shard_map/all_to_all | solution.py:317
  84.8 1.9 %collective-permute-start.2 = (bf16[4,8,64,512]{3,2,1,0:T(8,128)(2,1)S(1)}, bf16[4,8,64,512]{3,2,1,0:T(8,128)(2,1)S(1)}, u32[]{:S(2)}, u32[]{:S(2)}) collective-permute-start(bf16[4,8,64,512]{3,2,1,0:T(8,128)(2,1)S(1)} %all-to-all-done.1.w_ref), channel_id=1, source_target_pairs={{0,8},{8,0},{16,24},{24,16},{32,40},{40,32},{48,56},{56,48},{64,72... | collective-permute-start | bytes 6291464 | tf_op jit(solution)/shard_map/ppermute | solution.py:324
  86.7 1.6 %copy-done = bf16[2,8,256,256]{3,2,1,0:T(8,128)(2,1)S(1)} copy-done((bf16[2,8,256,256]{3,2,1,0:T(8,128)(2,1)S(1)}, bf16[2,8,256,256]{3,2,1,0:T(8,128)(2,1)}, u32[]{:S(2)}) %copy-start) | copy-done | bytes 2097176
  88.3 1.2 query_part.2.refs_0_
  89.5 1.3 collective-permute-done.2.w_ref
  90.8 1.2 query_part.3.q_ref
  92.7 14.3 %attend.2 = bf16[256,384]{1,0:T(8,128)(2,1)} custom-call(s32[3]{0:T(128)} %pad_add_fusion.s_ref, bf16[256,512]{1,0:T(8,128)(2,1)} %copy-done.1, bf16[2048,512]{1,0:T(8,128)(2,1)} %ko_ref.3, bf16[2048,512]{1,0:T(8,128)(2,1)} %vo_ref.3, bf16[2048,512]{1,0:T(8,128)(2,1)} %collective-permute-done.kf_ref, bf16[2048,512]{1,0:T(8,128)(2,1)} %collective-permute-done.1.vf_ref), custom_call_target="tpu_custom_call" | custom-call | flops 3221225472 | bytes 6291456 | tf_op jit(solution)/shard_map/attend/pallas_call | solution.py:264
  107.1 2.1 %collective-permute-start.3 = (bf16[4,8,64,512]{3,2,1,0:T(8,128)(2,1)}, bf16[4,8,64,512]{3,2,1,0:T(8,128)(2,1)S(1)}, u32[]{:S(2)}, u32[]{:S(2)}) collective-permute-start(bf16[4,8,64,512]{3,2,1,0:T(8,128)(2,1)} %bitcast.9), channel_id=1, source_target_pairs={{0,8},{8,0},{16,24},{24,16},{32,40},{40,32},{48,56},{56,48},{64,72... | collective-permute-start | bytes 6291464 | tf_op jit(solution)/shard_map/ppermute | solution.py:325
  109.2 7.1 %attend.3 = bf16[256,128]{1,0:T(8,128)(2,1)} custom-call(s32[3]{0:T(128)} %pad_add_fusion.s_ref, bf16[256,512]{1,0:T(8,128)(2,1)} %copy-done.1, bf16[2048,512]{1,0:T(8,128)(2,1)} %ko_ref.3, bf16[2048,512]{1,0:T(8,128)(2,1)} %vo_ref.3, bf16[2048,512]{1,0:T(8,128)(2,1)} %collective-permute-done.kf_ref, bf16[2048,512]{1,0:T(8,128)(2,1)} %collective-permute-done.1.vf_ref), custom_call_target="tpu_custom_call" | custom-call | flops 1073741824 | bytes 2097152 | tf_op jit(solution)/shard_map/attend/pallas_call | solution.py:264
  116.3 30.1 %all-gather.2 = bf16[2048,128]{1,0:T(8,128)(2,1)} all-gather(bf16[256,128]{1,0:T(8,128)(2,1)} %attend.3), channel_id=4, replica_groups=mesh['ctx'=64,'head'=8] {'head'}, dimensions={0}, use_global_device_ids=true | all-gather | bytes 589824 | tf_op jit(solution)/shard_map/all_gather | solution.py:334
  146.4 1.3 copy-done.2
  147.7 4.1 %output_product.1 = bf16[256,512]{1,0:T(8,128)(2,1)} custom-call(s32[1]{0:T(128)} %bitcast.5.side_ref, bf16[8,256,384]{2,1,0:T(8,128)(2,1)} %bitcast.13, bf16[8,256,128]{2,1,0:T(8,128)(2,1)} %bitcast.12, bf16[4,8,64,512]{3,2,1,0:T(8,128)(2,1)} %bitcast.10, bf16[4,8,64,512]{3,2,1,0:T(8,128)(2,1)} %copy-done.2), custom_call_target="tpu_custom_call" | custom-call | flops 1073741824 | bytes 6291456 | tf_op jit(solution)/shard_map/output_product/pallas_call | solution.py:164
  (20 shorter events, 2.1 us)
Async XLA Ops:
  6.5 53.3 %all-gather.8.cloned.1.call-start = ((), (), s32[]{:S(2)}) async-start(), calls=%async_computation.2 | async-start | bytes 2359296 | tf_op jit(solution)/shard_map/all_gather | solution.py:305
  9.3 39.0 %all-to-all-start = ((bf16[8,64,1024]{2,1,0:T(8,128)(2,1)}), bf16[8,64,1024]{2,1,0:T(8,128)(2,1)S(1)}, u32[]{:S(2)}, u32[]{:S(2)}) async-start(bf16[8,64,1024]{2,1,0:T(8,128)(2,1)} %broadcast_in_dim.9), calls=%async_computation | async-start | bytes 2097152 | tf_op jit(solution)/shard_map/all_to_all | solution.py:312
  19.6 44.9 %collective-permute-start = (bf16[2048,512]{1,0:T(8,128)(2,1)}, bf16[2048,512]{1,0:T(8,128)(2,1)}, u32[]{:S(2)}, u32[]{:S(2)}) collective-permute-start(bf16[2048,512]{1,0:T(8,128)(2,1)} %ko_ref.3), channel_id=1, source_target_pairs={{0,8},{8,0},{16,24},{24,16},{32,40},{40,32},{48,56},{56,48},{64,72... | collective-permute-start | bytes 6291464 | tf_op jit(solution)/shard_map/ppermute | solution.py:306
  21.5 42.9 %collective-permute-start.1 = (bf16[2048,512]{1,0:T(8,128)(2,1)}, bf16[2048,512]{1,0:T(8,128)(2,1)}, u32[]{:S(2)}, u32[]{:S(2)}) collective-permute-start(bf16[2048,512]{1,0:T(8,128)(2,1)} %vo_ref.3), channel_id=1, source_target_pairs={{0,8},{8,0},{16,24},{24,16},{32,40},{40,32},{48,56},{56,48},{64,72... | collective-permute-start | bytes 6291464 | tf_op jit(solution)/shard_map/ppermute | solution.py:307
  50.9 5.7 %copy-start.3 = (s32[32]{0:T(128)S(1)}, s32[32]{0:T(128)}, u32[]{:S(2)}) copy-start(s32[32]{0:T(128)} %param.15) | copy-start | bytes 388
  50.9 5.7 %copy-start.4 = (s32[32]{0:T(128)S(1)}, s32[32]{0:T(128)}, u32[]{:S(2)}) copy-start(s32[32]{0:T(128)} %param.14) | copy-start | bytes 388
  50.9 33.9 %all-to-all-start.1 = ((bf16[4,8,64,512]{3,2,1,0:T(8,128)(2,1)}), bf16[4,8,64,512]{3,2,1,0:T(8,128)(2,1)S(1)}, u32[]{:S(2)}, u32[]{:S(2)}) async-start(bf16[4,8,64,512]{3,2,1,0:T(8,128)(2,1)} %broadcast_in_dim.18), calls=%async_computation.1 | async-start | bytes 4194304 | tf_op jit(solution)/shard_map/all_to_all | solution.py:317
  55.8 51.3 %all-gather.12.cloned.1.call-start = ((), (), s32[]{:S(2)}) async-start(), calls=%async_computation.4 | async-start | bytes 2621440 | tf_op jit(solution)/shard_map/all_gather | solution.py:315
  56.5 89.9 %all-gather.10.cloned.1.call-start = ((), (), s32[]{:S(2)}) async-start(), calls=%async_computation.3 | async-start | bytes 1769472 | tf_op jit(solution)/shard_map/all_gather | solution.py:334
  84.8 6.0 %collective-permute-start.2 = (bf16[4,8,64,512]{3,2,1,0:T(8,128)(2,1)S(1)}, bf16[4,8,64,512]{3,2,1,0:T(8,128)(2,1)S(1)}, u32[]{:S(2)}, u32[]{:S(2)}) collective-permute-start(bf16[4,8,64,512]{3,2,1,0:T(8,128)(2,1)S(1)} %all-to-all-done.1.w_ref), channel_id=1, source_target_pairs={{0,8},{8,0},{16,24},{24,16},{32,40},{40,32},{48,56},{56,48},{64,72... | collective-permute-start | bytes 6291464 | tf_op jit(solution)/shard_map/ppermute | solution.py:324
  86.7 1.6 %copy-start = (bf16[2,8,256,256]{3,2,1,0:T(8,128)(2,1)S(1)}, bf16[2,8,256,256]{3,2,1,0:T(8,128)(2,1)}, u32[]{:S(2)}) copy-start(bf16[2,8,256,256]{3,2,1,0:T(8,128)(2,1)} %normalize.1.x_ref) | copy-start | bytes 6291460
  92.0 0.7 copy-start.1
  107.1 39.3 %collective-permute-start.3 = (bf16[4,8,64,512]{3,2,1,0:T(8,128)(2,1)}, bf16[4,8,64,512]{3,2,1,0:T(8,128)(2,1)S(1)}, u32[]{:S(2)}, u32[]{:S(2)}) collective-permute-start(bf16[4,8,64,512]{3,2,1,0:T(8,128)(2,1)} %bitcast.9), channel_id=1, source_target_pairs={{0,8},{8,0},{16,24},{24,16},{32,40},{40,32},{48,56},{56,48},{64,72... | collective-permute-start | bytes 6291464 | tf_op jit(solution)/shard_map/ppermute | solution.py:325
  146.4 1.3 copy-start.2
Sparse Core Ops, SparseCore 0:
  9.4 48.2 all-gather.7
  59.9 37.5 all-gather.11
  107.2 39.1 all-gather.9

commit v4 on v3

--- a/solution.py
+++ b/solution.py
@@ -14,6 +14,15 @@
 
 def place(x, z, core):
     return ((x % NX) * NZ + z % NZ) * 2 + core
+
+
+def along_x(shift):
+    return [
+        (place(x, z, core), place(x + shift, z, core))
+        for x in range(NX)
+        for z in range(NZ)
+        for core in range(2)
+    ]
 
 
 PARTNERS = [(i, i ^ 1) for i in range(2 * NX * NZ)]
@@ -130,7 +139,7 @@
     depth = NZ // each
     copies = []
     for i in range(NX):
-        blocks_of = slice(i * each, (i + 1) * each)
+        blocks_of = pl.ds(side_ref[1 + i] * each, each)
         group, at = [], 0
         for k, x_ref in enumerate(x_refs):
             lanes = slice(at, at + x_ref.shape[2])
@@ -138,9 +147,9 @@
                 pltpu.make_async_copy(x_ref.at[blocks_of], xs.at[blocks_of, :, lanes], sems.at[i, k])
             )
             at += x_ref.shape[2]
-        group.append(pltpu.make_async_copy(own_ref.at[i], w.at[i, :, core], sems.at[i, n_in]))
+        group.append(pltpu.make_async_copy(own_ref.at[:, i], w.at[i, :, core], sems.at[i, n_in]))
         group.append(
-            pltpu.make_async_copy(far_ref.at[i], w.at[i, :, 1 - core], sems.at[i, n_in + 1])
+            pltpu.make_async_copy(far_ref.at[:, i], w.at[i, :, 1 - core], sems.at[i, n_in + 1])
         )
         copies.append(group)
     for group in copies:
@@ -152,7 +161,8 @@
             copy.wait()
         for j in range(each):
             part = w[i, j * depth : (j + 1) * depth].reshape(width, o_ref.shape[1])
-            acc = acc + jnp.dot(xs[i * each + j], part, preferred_element_type=jnp.float32)
+            x = xs[side_ref[1 + i] * each + j]
+            acc = acc + jnp.dot(x, part, preferred_element_type=jnp.float32)
     o_ref[...] = acc.astype(jnp.bfloat16)
 
 
@@ -301,25 +311,26 @@
     ).astype(jnp.int32)
     own_side = core.reshape(1).astype(jnp.int32)
     far_side = 1 - own_side
+    x = position // (2 * NZ)
+    order = jnp.stack([core, x, (x - 1) % NX, (x + 1) % NX, (x + 2) % NX]).astype(jnp.int32)
 
     states = lax.all_gather(dec_states, "head")
     far_keys = lax.ppermute(enc_keys, "ctx", PARTNERS)
     far_values = lax.ppermute(enc_values, "ctx", PARTNERS)
 
-    pieces = jnp.broadcast_to(
-        jnp.concatenate([w_query, w_out], axis=1)[None], (NZ, piece, 2 * width)
-    )
-    pieces = lax.all_to_all(pieces, "ctx", 0, 0, axis_index_groups=Z_GROUPS)
-    wq = pieces[:, :, :width]
-    wo = pieces[:, :, width:]
-    wo_own = lax.all_gather(wo, "ctx", axis_index_groups=X_GROUPS)
+    wq = lax.all_to_all(
+        jnp.broadcast_to(w_query[None], (NZ, piece, width)), "ctx", 0, 0, axis_index_groups=Z_GROUPS
+    )
+    wo = jnp.stack([w_out] + [lax.ppermute(w_out, "ctx", along_x(shift)) for shift in (1, -1, 2)])
+    wq, wo = lax.optimization_barrier((wq, wo))
+    wo_own = lax.all_gather(wo, "ctx", axis_index_groups=Z_GROUPS)
 
     wq_own = lax.all_to_all(
         jnp.broadcast_to(wq[None], (NX, NZ, piece, width)), "ctx", 0, 0, axis_index_groups=X_GROUPS
     )
     normed = normalize(states, norm_gain.reshape(heads, 1, width))
-    wq_own, normed, far_keys, far_values, counts, own_side, far_side = lax.optimization_barrier(
-        (wq_own, normed, far_keys, far_values, counts, own_side, far_side)
+    wq_own, normed, far_keys, far_values, counts, own_side, far_side, order = lax.optimization_barrier(
+        (wq_own, normed, far_keys, far_values, counts, own_side, far_side, order)
     )
     wq_far = lax.ppermute(wq_own, "ctx", PARTNERS)
     wo_far = lax.ppermute(wo_own, "ctx", PARTNERS)
@@ -333,7 +344,7 @@
         )
         gathered.append(lax.all_gather(attended, "head"))
         start += pairs
-    return output_product(own_side, gathered, wo_own, wo_far)
+    return output_product(order, gathered, wo_own, wo_far)
 
 
 def solution(mesh):

time: 161 us -> 159 us (0.988); the launches traced: 158 us -> 158 us
  waiting for transfers between devices: 47.6 us -> 34.5 us
  starting transfers between devices: 23.5 us -> 36.1 us
    all_to_all x1, waiting for transfers between devices: 24.4 us -> 0.01 us  [local(): lax.all_to_all(jnp.broadcast_to(w_query[None], (NZ, piece, width)), 'ctx'...]
    all_to_all x1, waiting for transfers between devices: 20.3 us -> 7.83 us  [local(): lax.all_to_all(jnp.broadcast_to(wq[None], (NX, NZ, piece, width)), 'ctx',...]
    all_gather x1, waiting for transfers between devices: 0.02 us -> 10.7 us  [local(): wo_own = lax.all_gather(wo, 'ctx', axis_index_groups=Z_GROUPS)]
    ppermute x0 -> x3, starting transfers between devices: none -> 10.4 us  [local(): lax.ppermute(w_out, 'ctx', along_x(shift))]
    all_gather x1, waiting for transfers between devices: 0.01 us -> 6.24 us  [local(): states = lax.all_gather(dec_states, 'head')]
    all_gather x1, waiting for transfers between devices: 0.02 us -> 4.84 us  [local(): gathered.append(lax.all_gather(attended, 'head'))]
    all_to_all x1, starting transfers between devices: 4.9 us -> 7.18 us  [local(): lax.all_to_all(jnp.broadcast_to(wq[None], (NX, NZ, piece, width)), 'ctx',...]
    ppermute x0 -> x3, waiting for transfers between devices: none -> 2.19 us  [local(): lax.ppermute(w_out, 'ctx', along_x(shift))]
  transfers between devices with their start and end apart: 9 -> 12, of which waited for: 3 -> 7; matrix products, arithmetic and copies ran while one was open for 4% -> 4% of each run, Pallas kernels for 18% -> 18%
where the time goes in v4:
time: 159 us; the launch traced here: 158 us
  starting transfers between devices  36.1 us (23%)
  waiting for transfers between devices  34.5 us (22%)
  Pallas kernels  34 us (21%)
  blocking collectives  29.3 us (18%)
  between operations  15.2 us (10%)
  local copies, waits for them, and re-layouts  6.34 us (4%)
  other arithmetic  2.93 us (2%)
    all_gather x1, blocking collectives, local(): gathered.append(lax.all_gather(attended, 'head'))  29.3 us
    pallas_call x2, Pallas kernels, attend(): pl.pallas_call(functools.partial(attend_kernel, 512, start), out_shape=ja...  22.3 us
    all_gather x1, waiting for transfers between devices, local(): wo_own = lax.all_gather(wo, 'ctx', axis_index_groups=Z_GROUPS)  10.7 us
    ppermute x3, starting transfers between devices, local(): lax.ppermute(w_out, 'ctx', along_x(shift))  10.4 us
    all_to_all x1, starting transfers between devices, local(): lax.all_to_all(jnp.broadcast_to(w_query[None], (NZ, piece, width)), 'ctx'...  10.3 us
    all_to_all x1, waiting for transfers between devices, local(): lax.all_to_all(jnp.broadcast_to(wq[None], (NX, NZ, piece, width)), 'ctx',...  7.83 us
    all_to_all x1, starting transfers between devices, local(): lax.all_to_all(jnp.broadcast_to(wq[None], (NX, NZ, piece, width)), 'ctx',...  7.18 us
    all_gather x1, waiting for transfers between devices, local(): states = lax.all_gather(dec_states, 'head')  6.24 us
  transfers between devices with their start and end apart: 12, of which 7 were waited for; matrix products, arithmetic and copies ran while one was open for 4% of the time, Pallas kernels for 18%

profile of v4, /device:TPU:6, one launch (start us, length us, event | category | flops | bytes accessed | tf_op | source)
XLA Modules:
  0.0 158.4 jit_solution(1772841264697946823)
XLA Ops:
  7.3 1.7 %broadcast_in_dim.9 = bf16[8,64,512]{2,1,0:T(8,128)(2,1)} broadcast(bf16[64,512]{1,0:T(8,128)(2,1)} %param.10), dimensions={1,2} | broadcast | bytes 589824 | tf_op jit(solution)/shard_map/broadcast_in_dim | solution.py:322
  8.9 10.3 %all-to-all-start = ((bf16[8,64,512]{2,1,0:T(8,128)(2,1)}), bf16[8,64,512]{2,1,0:T(8,128)(2,1)S(1)}, u32[]{:S(2)}, u32[]{:S(2)}) async-start(bf16[8,64,512]{2,1,0:T(8,128)(2,1)} %broadcast_in_dim.9), calls=%async_computation | async-start | bytes 1048576 | tf_op jit(solution)/shard_map/all_to_all | solution.py:321
  19.2 1.9 %collective-permute-start.3 = (bf16[2048,512]{1,0:T(8,128)(2,1)}, bf16[2048,512]{1,0:T(8,128)(2,1)}, u32[]{:S(2)}, u32[]{:S(2)}) collective-permute-start(bf16[2048,512]{1,0:T(8,128)(2,1)} %ko_ref.3), channel_id=1, source_target_pairs={{0,8},{8,0},{16,24},{24,16},{32,40},{40,32},{48,56},{56,48},{64,72... | collective-permute-start | bytes 6291464 | tf_op jit(solution)/shard_map/ppermute | solution.py:318
  21.2 2.4 %collective-permute-start.4 = (bf16[2048,512]{1,0:T(8,128)(2,1)}, bf16[2048,512]{1,0:T(8,128)(2,1)}, u32[]{:S(2)}, u32[]{:S(2)}) collective-permute-start(bf16[2048,512]{1,0:T(8,128)(2,1)} %vo_ref.3), channel_id=1, source_target_pairs={{0,8},{8,0},{16,24},{24,16},{32,40},{40,32},{48,56},{56,48},{64,72... | collective-permute-start | bytes 6291464 | tf_op jit(solution)/shard_map/ppermute | solution.py:319
  23.6 3.3 %collective-permute-start.2 = (bf16[64,512]{1,0:T(8,128)(2,1)}, bf16[64,512]{1,0:T(8,128)(2,1)S(1)}, u32[]{:S(2)}, u32[]{:S(2)}) collective-permute-start(bf16[64,512]{1,0:T(8,128)(2,1)} %param.13), channel_id=1, source_target_pairs={{0,256},{8,264},{16,272},{24,280},{32,288},{40,296},{48,304},{56,3... | collective-permute-start | bytes 196616 | tf_op jit(solution)/shard_map/ppermute | solution.py:324
  26.9 1.9 %collective-permute-start.1 = (bf16[64,512]{1,0:T(8,128)(2,1)}, bf16[64,512]{1,0:T(8,128)(2,1)S(1)}, u32[]{:S(2)}, u32[]{:S(2)}) collective-permute-start(bf16[64,512]{1,0:T(8,128)(2,1)} %param.13), channel_id=1, source_target_pairs={{0,384},{8,392},{16,400},{24,408},{32,416},{40,424},{48,432},{56,4... | collective-permute-start | bytes 196616 | tf_op jit(solution)/shard_map/ppermute | solution.py:324
  28.8 5.1 %collective-permute-start = (bf16[64,512]{1,0:T(8,128)(2,1)}, bf16[64,512]{1,0:T(8,128)(2,1)S(1)}, u32[]{:S(2)}, u32[]{:S(2)}) collective-permute-start(bf16[64,512]{1,0:T(8,128)(2,1)} %param.13), channel_id=1, source_target_pairs={{0,128},{8,136},{16,144},{24,152},{32,160},{40,168},{48,176},{56,1... | collective-permute-start | bytes 196616 | tf_op jit(solution)/shard_map/ppermute | solution.py:324
  34.5 1.7 %collective-permute-done = bf16[64,512]{1,0:T(8,128)(2,1)S(1)} collective-permute-done((bf16[64,512]{1,0:T(8,128)(2,1)}, bf16[64,512]{1,0:T(8,128)(2,1)S(1)}, u32[]{:S(2)}, u32[]{:S(2)}) %collective-permute-start) | collective-permute-done | bytes 65568 | tf_op jit(solution)/shard_map/ppermute | solution.py:324
  36.2 1.6 %pad_maximum_fusion = bf16[4,64,512]{2,1,0:T(8,128)(2,1)} fusion(bf16[1,64,512]{2,1,0:T(8,128)(2,1)S(1)} %bitcast.23, bf16[1,64,512]{2,1,0:T(8,128)(2,1)S(1)} %bitcast.24, bf16[1,64,512]{2,1,0:T(8,128)(2,1)S(1)} %bitcast.25, bf16[1,64,512]{2,1,0:T(8,128)(2,1)} %bitcast.22), kind=kLoop, calls=%fused_computation | loop fusion | flops 393216 | bytes 524288 | tf_op jit(solution)/shard_map/stack | solution.py:324
  37.8 1.6 %broadcast_in_dim.18 = bf16[4,8,64,512]{3,2,1,0:T(8,128)(2,1)} broadcast(bf16[8,64,512]{2,1,0:T(8,128)(2,1)S(1)} %all-to-all-done), dimensions={1,2,3} | broadcast | bytes 2621440 | tf_op jit(solution)/shard_map/broadcast_in_dim | solution.py:329
  39.4 7.2 %all-to-all-start.1 = ((bf16[4,8,64,512]{3,2,1,0:T(8,128)(2,1)}), bf16[4,8,64,512]{3,2,1,0:T(8,128)(2,1)S(1)}, u32[]{:S(2)}, u32[]{:S(2)}) async-start(bf16[4,8,64,512]{3,2,1,0:T(8,128)(2,1)} %broadcast_in_dim.18), calls=%async_computation.1 | async-start | bytes 4194304 | tf_op jit(solution)/shard_map/all_to_all | solution.py:328
  51.4 6.2 %all-gather.8.cloned.1.call-done = bf16[2048,512]{1,0:T(8,128)(2,1)} async-done(((bf16[256,512]{1,0:T(8,128)(2,1)}), bf16[2048,512]{1,0:T(8,128)(2,1)}) %all-gather.8.cloned.1.call-update) | async-done | bytes 2097168 | tf_op jit(solution)/shard_map/all_gather | solution.py:317
  57.6 4.6 %normalize.1.x_ref = bf16[2,8,256,256]{3,2,1,0:T(8,128)(2,1)} custom-call(bf16[8,256,512]{2,1,0:T(8,128)(2,1)} %bitcast.17, f32[8,1,512]{2,1,0:T(1,128)} %bitcast.26), custom_call_target="tpu_custom_call" | custom-call | flops 8388608 | bytes 4194304 | tf_op jit(solution)/shard_map/normalize/pallas_call | solution.py:57
  62.2 7.8 %all-to-all-done.1.w_ref = bf16[4,8,64,512]{3,2,1,0:T(8,128)(2,1)S(1)} async-done(((bf16[4,8,64,512]{3,2,1,0:T(8,128)(2,1)}), bf16[4,8,64,512]{3,2,1,0:T(8,128)(2,1)S(1)}, u32[]{:S(2)}, u32[]{:S(2)}) %all-to-all-start.1) | async-done | bytes 2097184 | tf_op jit(solution)/shard_map/all_to_all | solution.py:328
  70.0 1.9 %collective-permute-start.5 = (bf16[4,8,64,512]{3,2,1,0:T(8,128)(2,1)S(1)}, bf16[4,8,64,512]{3,2,1,0:T(8,128)(2,1)S(1)}, u32[]{:S(2)}, u32[]{:S(2)}) collective-permute-start(bf16[4,8,64,512]{3,2,1,0:T(8,128)(2,1)S(1)} %all-to-all-done.1.w_ref), channel_id=1, source_target_pairs={{0,8},{8,0},{16,24},{24,16},{32,40},{40,32},{48,56},{56,48},{64,72... | collective-permute-start | bytes 6291464 | tf_op jit(solution)/shard_map/ppermute | solution.py:335
  71.9 1.7 %copy-done = bf16[2,8,256,256]{3,2,1,0:T(8,128)(2,1)S(1)} copy-done((bf16[2,8,256,256]{3,2,1,0:T(8,128)(2,1)S(1)}, bf16[2,8,256,256]{3,2,1,0:T(8,128)(2,1)}, u32[]{:S(2)}) %copy-start) | copy-done | bytes 2097176
  74.8 1.3 collective-permute-done.5.w_ref
  77.9 14.9 %attend.2 = bf16[256,384]{1,0:T(8,128)(2,1)} custom-call(s32[3]{0:T(128)} %pad_add_fusion.s_ref, bf16[256,512]{1,0:T(8,128)(2,1)} %copy-done.1, bf16[2048,512]{1,0:T(8,128)(2,1)} %ko_ref.3, bf16[2048,512]{1,0:T(8,128)(2,1)} %vo_ref.3, bf16[2048,512]{1,0:T(8,128)(2,1)} %collective-permute-done.3.kf_ref, bf16[2048,512]{1,0:T(8,128)(2,1)} %collective-permute-done.4.vf_ref), custom_call_target="tpu_custom_call" | custom-call | flops 3221225472 | bytes 6291456 | tf_op jit(solution)/shard_map/attend/pallas_call | solution.py:274
  92.9 10.7 %all-gather.12.cloned.1.call-done = bf16[32,64,512]{2,1,0:T(8,128)(2,1)} async-done(((bf16[4,64,512]{2,1,0:T(8,128)(2,1)}), bf16[32,64,512]{2,1,0:T(8,128)(2,1)}) %all-gather.12.cloned.1.call-update) | async-done | bytes 2097168 | tf_op jit(solution)/shard_map/all_gather | solution.py:326
  103.5 1.9 %collective-permute-start.6 = (bf16[8,4,64,512]{3,2,1,0:T(8,128)(2,1)}, bf16[8,4,64,512]{3,2,1,0:T(8,128)(2,1)S(1)}, u32[]{:S(2)}, u32[]{:S(2)}) collective-permute-start(bf16[8,4,64,512]{3,2,1,0:T(8,128)(2,1)} %bitcast.18), channel_id=1, source_target_pairs={{0,8},{8,0},{16,24},{24,16},{32,40},{40,32},{48,56},{56,48},{64,72... | collective-permute-start | bytes 6291464 | tf_op jit(solution)/shard_map/ppermute | solution.py:336
  105.5 7.4 %attend.3 = bf16[256,128]{1,0:T(8,128)(2,1)} custom-call(s32[3]{0:T(128)} %pad_add_fusion.s_ref, bf16[256,512]{1,0:T(8,128)(2,1)} %copy-done.1, bf16[2048,512]{1,0:T(8,128)(2,1)} %ko_ref.3, bf16[2048,512]{1,0:T(8,128)(2,1)} %vo_ref.3, bf16[2048,512]{1,0:T(8,128)(2,1)} %collective-permute-done.3.kf_ref, bf16[2048,512]{1,0:T(8,128)(2,1)} %collective-permute-done.4.vf_ref), custom_call_target="tpu_custom_call" | custom-call | flops 1073741824 | bytes 2097152 | tf_op jit(solution)/shard_map/attend/pallas_call | solution.py:274
  112.9 29.3 %all-gather.2 = bf16[2048,128]{1,0:T(8,128)(2,1)} all-gather(bf16[256,128]{1,0:T(8,128)(2,1)} %attend.3), channel_id=4, replica_groups=mesh['ctx'=64,'head'=8] {'head'}, dimensions={0}, use_global_device_ids=true | all-gather | bytes 589824 | tf_op jit(solution)/shard_map/all_gather | solution.py:345
  142.3 4.8 %all-gather.10.cloned.1.call-done = bf16[2048,384]{1,0:T(8,128)(2,1)} async-done(((bf16[256,384]{1,0:T(8,128)(2,1)}), bf16[2048,384]{1,0:T(8,128)(2,1)}) %all-gather.10.cloned.1.call-update) | async-done | bytes 1572880 | tf_op jit(solution)/shard_map/all_gather | solution.py:345
  147.1 4.7 %output_product.1 = bf16[256,512]{1,0:T(8,128)(2,1)} custom-call(s32[5]{0:T(128)} %stack.56.side_ref, bf16[8,256,384]{2,1,0:T(8,128)(2,1)} %bitcast.21, bf16[8,256,128]{2,1,0:T(8,128)(2,1)} %bitcast.20, bf16[8,4,64,512]{3,2,1,0:T(8,128)(2,1)} %bitcast.19, bf16[8,4,64,512]{3,2,1,0:T(8,128)(2,1)} %copy-done.2), custom_call_target="tpu_custom_call" | custom-call | flops 1073741824 | bytes 6291456 | tf_op jit(solution)/shard_map/output_product/pallas_call | solution.py:174
  (26 shorter events, 7.0 us)
Async XLA Ops:
  6.5 51.1 %all-gather.8.cloned.1.call-start = ((), (), s32[]{:S(2)}) async-start(), calls=%async_computation.2 | async-start | bytes 2359296 | tf_op jit(solution)/shard_map/all_gather | solution.py:317
  8.9 28.8 %all-to-all-start = ((bf16[8,64,512]{2,1,0:T(8,128)(2,1)}), bf16[8,64,512]{2,1,0:T(8,128)(2,1)S(1)}, u32[]{:S(2)}, u32[]{:S(2)}) async-start(bf16[8,64,512]{2,1,0:T(8,128)(2,1)} %broadcast_in_dim.9), calls=%async_computation | async-start | bytes 1048576 | tf_op jit(solution)/shard_map/all_to_all | solution.py:321
  19.2 42.9 %collective-permute-start.3 = (bf16[2048,512]{1,0:T(8,128)(2,1)}, bf16[2048,512]{1,0:T(8,128)(2,1)}, u32[]{:S(2)}, u32[]{:S(2)}) collective-permute-start(bf16[2048,512]{1,0:T(8,128)(2,1)} %ko_ref.3), channel_id=1, source_target_pairs={{0,8},{8,0},{16,24},{24,16},{32,40},{40,32},{48,56},{56,48},{64,72... | collective-permute-start | bytes 6291464 | tf_op jit(solution)/shard_map/ppermute | solution.py:318
  21.2 41.0 %collective-permute-start.4 = (bf16[2048,512]{1,0:T(8,128)(2,1)}, bf16[2048,512]{1,0:T(8,128)(2,1)}, u32[]{:S(2)}, u32[]{:S(2)}) collective-permute-start(bf16[2048,512]{1,0:T(8,128)(2,1)} %vo_ref.3), channel_id=1, source_target_pairs={{0,8},{8,0},{16,24},{24,16},{32,40},{40,32},{48,56},{56,48},{64,72... | collective-permute-start | bytes 6291464 | tf_op jit(solution)/shard_map/ppermute | solution.py:319
  23.6 10.4 %collective-permute-start.2 = (bf16[64,512]{1,0:T(8,128)(2,1)}, bf16[64,512]{1,0:T(8,128)(2,1)S(1)}, u32[]{:S(2)}, u32[]{:S(2)}) collective-permute-start(bf16[64,512]{1,0:T(8,128)(2,1)} %param.13), channel_id=1, source_target_pairs={{0,256},{8,264},{16,272},{24,280},{32,288},{40,296},{48,304},{56,3... | collective-permute-start | bytes 196616 | tf_op jit(solution)/shard_map/ppermute | solution.py:324
  26.9 7.6 %collective-permute-start.1 = (bf16[64,512]{1,0:T(8,128)(2,1)}, bf16[64,512]{1,0:T(8,128)(2,1)S(1)}, u32[]{:S(2)}, u32[]{:S(2)}) collective-permute-start(bf16[64,512]{1,0:T(8,128)(2,1)} %param.13), channel_id=1, source_target_pairs={{0,384},{8,392},{16,400},{24,408},{32,416},{40,424},{48,432},{56,4... | collective-permute-start | bytes 196616 | tf_op jit(solution)/shard_map/ppermute | solution.py:324
  28.8 7.3 %collective-permute-start = (bf16[64,512]{1,0:T(8,128)(2,1)}, bf16[64,512]{1,0:T(8,128)(2,1)S(1)}, u32[]{:S(2)}, u32[]{:S(2)}) collective-permute-start(bf16[64,512]{1,0:T(8,128)(2,1)} %param.13), channel_id=1, source_target_pairs={{0,128},{8,136},{16,144},{24,152},{32,160},{40,168},{48,176},{56,1... | collective-permute-start | bytes 196616 | tf_op jit(solution)/shard_map/ppermute | solution.py:324
  39.4 8.0 %copy-start.3 = (s32[32]{0:T(128)S(1)}, s32[32]{0:T(128)}, u32[]{:S(2)}) copy-start(s32[32]{0:T(128)} %param.15) | copy-start | bytes 388
  39.4 8.1 %copy-start.4 = (s32[32]{0:T(128)S(1)}, s32[32]{0:T(128)}, u32[]{:S(2)}) copy-start(s32[32]{0:T(128)} %param.14) | copy-start | bytes 388
  39.4 30.6 %all-to-all-start.1 = ((bf16[4,8,64,512]{3,2,1,0:T(8,128)(2,1)}), bf16[4,8,64,512]{3,2,1,0:T(8,128)(2,1)S(1)}, u32[]{:S(2)}, u32[]{:S(2)}) async-start(bf16[4,8,64,512]{3,2,1,0:T(8,128)(2,1)} %broadcast_in_dim.18), calls=%async_computation.1 | async-start | bytes 4194304 | tf_op jit(solution)/shard_map/all_to_all | solution.py:328
  46.6 56.9 %all-gather.12.cloned.1.call-start = ((), (), s32[]{:S(2)}) async-start(), calls=%async_computation.4 | async-start | bytes 2359296 | tf_op jit(solution)/shard_map/all_gather | solution.py:326
  47.3 99.8 %all-gather.10.cloned.1.call-start = ((), (), s32[]{:S(2)}) async-start(), calls=%async_computation.3 | async-start | bytes 1769472 | tf_op jit(solution)/shard_map/all_gather | solution.py:345
  70.0 6.0 %collective-permute-start.5 = (bf16[4,8,64,512]{3,2,1,0:T(8,128)(2,1)S(1)}, bf16[4,8,64,512]{3,2,1,0:T(8,128)(2,1)S(1)}, u32[]{:S(2)}, u32[]{:S(2)}) collective-permute-start(bf16[4,8,64,512]{3,2,1,0:T(8,128)(2,1)S(1)} %all-to-all-done.1.w_ref), channel_id=1, source_target_pairs={{0,8},{8,0},{16,24},{24,16},{32,40},{40,32},{48,56},{56,48},{64,72... | collective-permute-start | bytes 6291464 | tf_op jit(solution)/shard_map/ppermute | solution.py:335
  71.9 1.7 %copy-start = (bf16[2,8,256,256]{3,2,1,0:T(8,128)(2,1)S(1)}, bf16[2,8,256,256]{3,2,1,0:T(8,128)(2,1)}, u32[]{:S(2)}) copy-start(bf16[2,8,256,256]{3,2,1,0:T(8,128)(2,1)} %normalize.1.x_ref) | copy-start | bytes 6291460
  77.2 0.7 copy-start.1
  103.5 38.7 %collective-permute-start.6 = (bf16[8,4,64,512]{3,2,1,0:T(8,128)(2,1)}, bf16[8,4,64,512]{3,2,1,0:T(8,128)(2,1)S(1)}, u32[]{:S(2)}, u32[]{:S(2)}) collective-permute-start(bf16[8,4,64,512]{3,2,1,0:T(8,128)(2,1)} %bitcast.18), channel_id=1, source_target_pairs={{0,8},{8,0},{16,24},{24,16},{32,40},{40,32},{48,56},{56,48},{64,72... | collective-permute-start | bytes 6291464 | tf_op jit(solution)/shard_map/ppermute | solution.py:336
  142.3 4.8 %copy-start.2 = (bf16[8,4,64,512]{3,2,1,0:T(8,128)(2,1)}, bf16[8,4,64,512]{3,2,1,0:T(8,128)(2,1)S(1)}, u32[]{:S(2)}) copy-start(bf16[8,4,64,512]{3,2,1,0:T(8,128)(2,1)S(1)} %collective-permute-done.6.refs_3_) | copy-start | bytes 6291460
Sparse Core Ops, SparseCore 0:
  9.4 48.1 all-gather.7
  59.7 43.8 all-gather.11
  105.6 41.4 all-gather.9

commit v5 on v4

--- a/solution.py
+++ b/solution.py
@@ -9,7 +9,7 @@
 
 DK = 64
 NX, NZ = 4, 8
-CUTS = (3, 1)
+CUTS = (144, 112)
 
 
 def place(x, z, core):
@@ -142,11 +142,11 @@
         blocks_of = pl.ds(side_ref[1 + i] * each, each)
         group, at = [], 0
         for k, x_ref in enumerate(x_refs):
-            lanes = slice(at, at + x_ref.shape[2])
+            part = slice(at, at + x_ref.shape[1])
             group.append(
-                pltpu.make_async_copy(x_ref.at[blocks_of], xs.at[blocks_of, :, lanes], sems.at[i, k])
+                pltpu.make_async_copy(x_ref.at[blocks_of], xs.at[blocks_of, part], sems.at[i, k])
             )
-            at += x_ref.shape[2]
+            at += x_ref.shape[1]
         group.append(pltpu.make_async_copy(own_ref.at[:, i], w.at[i, :, core], sems.at[i, n_in]))
         group.append(
             pltpu.make_async_copy(far_ref.at[:, i], w.at[i, :, 1 - core], sems.at[i, n_in + 1])
@@ -167,8 +167,8 @@
 
 
 def output_product(side, xs, own, far):
-    blocks, rows = xs[0].shape[:2]
-    width = sum(x.shape[2] for x in xs)
+    blocks, _, width = xs[0].shape
+    rows = sum(x.shape[1] for x in xs)
     piece, out = own.shape[2:]
     anywhere = pl.BlockSpec(memory_space=pl.ANY)
     return pl.pallas_call(
@@ -195,7 +195,8 @@
     )(side, *xs, own, far)
 
 
-def attend_kernel(step, start, s_ref, q_ref, ko_ref, vo_ref, kf_ref, vf_ref, o_ref, keys, vals, sems):
+def attend_kernel(step, s_ref, q_ref, ko_ref, vo_ref, kf_ref, vf_ref, *refs):
+    *o_refs, keys, vals, sems = refs
     half = ko_ref.shape[0]
     rows = q_ref.shape[0]
     pair, tile = 2 * DK, 256
@@ -203,7 +204,7 @@
     slot = lax.rem(turn, 2)
 
     def copies(h, into):
-        lanes = pl.ds(pl.multiple_of((start + h) * pair, pair), pair)
+        lanes = pl.ds(pl.multiple_of(h * pair, pair), pair)
         return [
             pltpu.make_async_copy(ko_ref.at[:, lanes], keys.at[into, :half], sems.at[into, 0]),
             pltpu.make_async_copy(kf_ref.at[:, lanes], keys.at[into, half:], sems.at[into, 1]),
@@ -260,23 +261,26 @@
         top = new_top
     out = acc[:, :pair] / acc[:, pair:]
     live = lax.broadcasted_iota(jnp.int32, (rows, 1), 0) < s_ref[2]
-    o_ref[...] = jnp.where(live, jnp.where(first, out[:rows], out[rows:]), 0.0).astype(jnp.bfloat16)
-
-
-def attend(counts, q, own_k, own_v, far_k, far_v, start, pairs):
-    rows = q.shape[0]
-    width = pairs * 2 * DK
+    out = jnp.where(live, jnp.where(first, out[:rows], out[rows:]), 0.0).astype(jnp.bfloat16)
+    at = 0
+    for o_ref in o_refs:
+        o_ref[...] = out[at : at + o_ref.shape[0]]
+        at += o_ref.shape[0]
+
+
+def attend(counts, q, own_k, own_v, far_k, far_v, cuts):
+    rows, width = q.shape
     half = own_k.shape[0]
     pair = 2 * DK
     hbm = pl.BlockSpec(memory_space=pl.ANY)
-    qs = pl.BlockSpec((rows, pair), lambda h, s: (0, start + h))
-    os = pl.BlockSpec((rows, pair), lambda h, s: (0, h))
+    qs = pl.BlockSpec((rows, pair), lambda h, s: (0, h))
+    os = [pl.BlockSpec((cut, pair), lambda h, s: (0, h)) for cut in cuts]
     return pl.pallas_call(
-        functools.partial(attend_kernel, 512, start),
-        out_shape=jax.ShapeDtypeStruct((rows, width), jnp.bfloat16),
+        functools.partial(attend_kernel, 512),
+        out_shape=[jax.ShapeDtypeStruct((cut, width), jnp.bfloat16) for cut in cuts],
         grid_spec=pltpu.PrefetchScalarGridSpec(
             num_scalar_prefetch=1,
-            grid=(pairs,),
+            grid=(width // pair,),
             in_specs=[qs, hbm, hbm, hbm, hbm],
             out_specs=os,
             scratch_shapes=[
@@ -333,17 +337,13 @@
         (wq_own, normed, far_keys, far_values, counts, own_side, far_side, order)
     )
     wq_far = lax.ppermute(wq_own, "ctx", PARTNERS)
-    wo_far = lax.ppermute(wo_own, "ctx", PARTNERS)
 
     queries = query_part(own_side, normed, wq_own)
     queries = query_part(far_side, normed, wq_far, queries)
-    gathered, start = [], 0
-    for pairs in CUTS:
-        attended = attend(
-            counts, queries, enc_keys, enc_values, far_keys, far_values, start, pairs
-        )
-        gathered.append(lax.all_gather(attended, "head"))
-        start += pairs
+    attended = attend(counts, queries, enc_keys, enc_values, far_keys, far_values, CUTS)
+    gathered = [lax.all_gather(part, "head") for part in attended]
+    wo_own, _ = lax.optimization_barrier((wo_own, attended[1]))
+    wo_far = lax.ppermute(wo_own, "ctx", PARTNERS)
     return output_product(order, gathered, wo_own, wo_far)
 
 

time: 159 us -> 160 us (level)
  Pallas kernels: 34 us -> 29.9 us
    all_gather x1, waiting for transfers between devices: 4.84 us -> 9.45 us  [local(): gathered = [lax.all_gather(part, 'head') for part in attended]]
    pallas_call x2 -> x1, Pallas kernels: 22.3 us -> 18.3 us  [attend(): pl.pallas_call(functools.partial(attend_kernel, 512), out_shape=[jax.Shap...]
    all_gather x1, waiting for transfers between devices: 10.7 us -> 7.29 us  [local(): wo_own = lax.all_gather(wo, 'ctx', axis_index_groups=Z_GROUPS)]
  transfers between devices with their start and end apart: 12 -> 12, of which waited for: 7 -> 7; matrix products, arithmetic and copies ran while one was open for 4% -> 4% of each run, Pallas kernels for 18% -> 16%
where the time goes in v5:
time: 160 us; the launch traced here: 158 us
  starting transfers between devices  36.1 us (23%)
  waiting for transfers between devices  35.8 us (22%)
  blocking collectives  30.9 us (19%)
  Pallas kernels  29.9 us (19%)
  between operations  15.2 us (10%)
  local copies, waits for them, and re-layouts  7.67 us (5%)
  other arithmetic  2.98 us (2%)
    all_gather x1, blocking collectives, local(): gathered = [lax.all_gather(part, 'head') for part in attended]  30.9 us
    pallas_call x1, Pallas kernels, attend(): pl.pallas_call(functools.partial(attend_kernel, 512), out_shape=[jax.Shap...  18.3 us
    ppermute x3, starting transfers between devices, local(): lax.ppermute(w_out, 'ctx', along_x(shift))  10.4 us
    all_to_all x1, starting transfers between devices, local(): lax.all_to_all(jnp.broadcast_to(w_query[None], (NZ, piece, width)), 'ctx'...  10.3 us
    all_gather x1, waiting for transfers between devices, local(): gathered = [lax.all_gather(part, 'head') for part in attended]  9.45 us
    all_to_all x1, waiting for transfers between devices, local(): lax.all_to_all(jnp.broadcast_to(wq[None], (NX, NZ, piece, width)), 'ctx',...  7.81 us
    all_gather x1, waiting for transfers between devices, local(): wo_own = lax.all_gather(wo, 'ctx', axis_index_groups=Z_GROUPS)  7.29 us
    all_to_all x1, starting transfers between devices, local(): lax.all_to_all(jnp.broadcast_to(wq[None], (NX, NZ, piece, width)), 'ctx',...  7.19 us
  transfers between devices with their start and end apart: 12, of which 7 were waited for; matrix products, arithmetic and copies ran while one was open for 4% of the time, Pallas kernels for 16%

profile of v5, /device:TPU:6, one launch (start us, length us, event | category | flops | bytes accessed | tf_op | source)
XLA Modules:
  0.0 158.4 jit_solution(678469552998145400)
XLA Ops:
  7.3 1.7 %broadcast_in_dim.9 = bf16[8,64,512]{2,1,0:T(8,128)(2,1)} broadcast(bf16[64,512]{1,0:T(8,128)(2,1)} %param.10), dimensions={1,2} | broadcast | bytes 589824 | tf_op jit(solution)/shard_map/broadcast_in_dim | solution.py:326
  8.9 10.3 %all-to-all-start = ((bf16[8,64,512]{2,1,0:T(8,128)(2,1)}), bf16[8,64,512]{2,1,0:T(8,128)(2,1)S(1)}, u32[]{:S(2)}, u32[]{:S(2)}) async-start(bf16[8,64,512]{2,1,0:T(8,128)(2,1)} %broadcast_in_dim.9), calls=%async_computation | async-start | bytes 1048576 | tf_op jit(solution)/shard_map/all_to_all | solution.py:325
  19.3 1.9 %collective-permute-start.3 = (bf16[2048,512]{1,0:T(8,128)(2,1)}, bf16[2048,512]{1,0:T(8,128)(2,1)}, u32[]{:S(2)}, u32[]{:S(2)}) collective-permute-start(bf16[2048,512]{1,0:T(8,128)(2,1)} %ko_ref.1), channel_id=1, source_target_pairs={{0,8},{8,0},{16,24},{24,16},{32,40},{40,32},{48,56},{56,48},{64,72... | collective-permute-start | bytes 6291464 | tf_op jit(solution)/shard_map/ppermute | solution.py:322
  21.2 2.4 %collective-permute-start.4 = (bf16[2048,512]{1,0:T(8,128)(2,1)}, bf16[2048,512]{1,0:T(8,128)(2,1)}, u32[]{:S(2)}, u32[]{:S(2)}) collective-permute-start(bf16[2048,512]{1,0:T(8,128)(2,1)} %vo_ref.1), channel_id=1, source_target_pairs={{0,8},{8,0},{16,24},{24,16},{32,40},{40,32},{48,56},{56,48},{64,72... | collective-permute-start | bytes 6291464 | tf_op jit(solution)/shard_map/ppermute | solution.py:323
  23.6 3.3 %collective-permute-start.2 = (bf16[64,512]{1,0:T(8,128)(2,1)}, bf16[64,512]{1,0:T(8,128)(2,1)S(1)}, u32[]{:S(2)}, u32[]{:S(2)}) collective-permute-start(bf16[64,512]{1,0:T(8,128)(2,1)} %param.13), channel_id=1, source_target_pairs={{0,256},{8,264},{16,272},{24,280},{32,288},{40,296},{48,304},{56,3... | collective-permute-start | bytes 196616 | tf_op jit(solution)/shard_map/ppermute | solution.py:328
  26.9 1.9 %collective-permute-start.1 = (bf16[64,512]{1,0:T(8,128)(2,1)}, bf16[64,512]{1,0:T(8,128)(2,1)S(1)}, u32[]{:S(2)}, u32[]{:S(2)}) collective-permute-start(bf16[64,512]{1,0:T(8,128)(2,1)} %param.13), channel_id=1, source_target_pairs={{0,384},{8,392},{16,400},{24,408},{32,416},{40,424},{48,432},{56,4... | collective-permute-start | bytes 196616 | tf_op jit(solution)/shard_map/ppermute | solution.py:328
  28.9 5.1 %collective-permute-start = (bf16[64,512]{1,0:T(8,128)(2,1)}, bf16[64,512]{1,0:T(8,128)(2,1)S(1)}, u32[]{:S(2)}, u32[]{:S(2)}) collective-permute-start(bf16[64,512]{1,0:T(8,128)(2,1)} %param.13), channel_id=1, source_target_pairs={{0,128},{8,136},{16,144},{24,152},{32,160},{40,168},{48,176},{56,1... | collective-permute-start | bytes 196616 | tf_op jit(solution)/shard_map/ppermute | solution.py:328
  34.5 1.7 %collective-permute-done = bf16[64,512]{1,0:T(8,128)(2,1)S(1)} collective-permute-done((bf16[64,512]{1,0:T(8,128)(2,1)}, bf16[64,512]{1,0:T(8,128)(2,1)S(1)}, u32[]{:S(2)}, u32[]{:S(2)}) %collective-permute-start) | collective-permute-done | bytes 65568 | tf_op jit(solution)/shard_map/ppermute | solution.py:328
  36.2 1.6 %pad_maximum_fusion = bf16[4,64,512]{2,1,0:T(8,128)(2,1)} fusion(bf16[1,64,512]{2,1,0:T(8,128)(2,1)S(1)} %bitcast.23, bf16[1,64,512]{2,1,0:T(8,128)(2,1)S(1)} %bitcast.24, bf16[1,64,512]{2,1,0:T(8,128)(2,1)S(1)} %bitcast.25, bf16[1,64,512]{2,1,0:T(8,128)(2,1)} %bitcast.22), kind=kLoop, calls=%fused_computation | loop fusion | flops 393216 | bytes 524288 | tf_op jit(solution)/shard_map/stack | solution.py:328
  37.8 1.6 %broadcast_in_dim.18 = bf16[4,8,64,512]{3,2,1,0:T(8,128)(2,1)} broadcast(bf16[8,64,512]{2,1,0:T(8,128)(2,1)S(1)} %all-to-all-done), dimensions={1,2,3} | broadcast | bytes 2621440 | tf_op jit(solution)/shard_map/broadcast_in_dim | solution.py:333
  39.4 7.2 %all-to-all-start.1 = ((bf16[4,8,64,512]{3,2,1,0:T(8,128)(2,1)}), bf16[4,8,64,512]{3,2,1,0:T(8,128)(2,1)S(1)}, u32[]{:S(2)}, u32[]{:S(2)}) async-start(bf16[4,8,64,512]{3,2,1,0:T(8,128)(2,1)} %broadcast_in_dim.18), calls=%async_computation.1 | async-start | bytes 4194304 | tf_op jit(solution)/shard_map/all_to_all | solution.py:332
  51.4 6.3 %all-gather.8.cloned.1.call-done = bf16[2048,512]{1,0:T(8,128)(2,1)} async-done(((bf16[256,512]{1,0:T(8,128)(2,1)}), bf16[2048,512]{1,0:T(8,128)(2,1)}) %all-gather.8.cloned.1.call-update) | async-done | bytes 2097168 | tf_op jit(solution)/shard_map/all_gather | solution.py:321
  57.7 4.5 %normalize.1.x_ref = bf16[2,8,256,256]{3,2,1,0:T(8,128)(2,1)} custom-call(bf16[8,256,512]{2,1,0:T(8,128)(2,1)} %bitcast.18, f32[8,1,512]{2,1,0:T(1,128)} %bitcast.26), custom_call_target="tpu_custom_call" | custom-call | flops 8388608 | bytes 4194304 | tf_op jit(solution)/shard_map/normalize/pallas_call | solution.py:57
  62.2 7.8 %all-to-all-done.1.w_ref = bf16[4,8,64,512]{3,2,1,0:T(8,128)(2,1)S(1)} async-done(((bf16[4,8,64,512]{3,2,1,0:T(8,128)(2,1)}), bf16[4,8,64,512]{3,2,1,0:T(8,128)(2,1)S(1)}, u32[]{:S(2)}, u32[]{:S(2)}) %all-to-all-start.1) | async-done | bytes 2097184 | tf_op jit(solution)/shard_map/all_to_all | solution.py:332
  70.0 1.9 %collective-permute-start.5 = (bf16[4,8,64,512]{3,2,1,0:T(8,128)(2,1)S(1)}, bf16[4,8,64,512]{3,2,1,0:T(8,128)(2,1)S(1)}, u32[]{:S(2)}, u32[]{:S(2)}) collective-permute-start(bf16[4,8,64,512]{3,2,1,0:T(8,128)(2,1)S(1)} %all-to-all-done.1.w_ref), channel_id=1, source_target_pairs={{0,8},{8,0},{16,24},{24,16},{32,40},{40,32},{48,56},{56,48},{64,72... | collective-permute-start | bytes 6291464 | tf_op jit(solution)/shard_map/ppermute | solution.py:339
  72.0 1.7 %copy-done = bf16[2,8,256,256]{3,2,1,0:T(8,128)(2,1)S(1)} copy-done((bf16[2,8,256,256]{3,2,1,0:T(8,128)(2,1)S(1)}, bf16[2,8,256,256]{3,2,1,0:T(8,128)(2,1)}, u32[]{:S(2)}) %copy-start) | copy-done | bytes 2097176
  74.8 1.3 collective-permute-done.5.w_ref
  78.0 18.3 %attend.1 = (bf16[144,512]{1,0:T(8,128)(2,1)}, bf16[112,512]{1,0:T(8,128)(2,1)}) custom-call(s32[3]{0:T(128)} %pad_add_fusion.s_ref, bf16[256,512]{1,0:T(8,128)(2,1)} %copy-done.1, bf16[2048,512]{1,0:T(8,128)(2,1)} %ko_ref.1, bf16[2048,512]{1,0:T(8,128)(2,1)} %vo_ref.1, bf16[2048,512]{1,0:T(8,128)(2,1)} %collective-permute-done.3.kf_ref, ...), custom_call_target="tpu_custom_call" | custom-call | flops 4294967296 | bytes 8388608 | tf_op jit(solution)/shard_map/attend/pallas_call | solution.py:278
  96.3 7.3 %all-gather.12.cloned.1.call-done = bf16[32,64,512]{2,1,0:T(8,128)(2,1)} async-done(((bf16[4,64,512]{2,1,0:T(8,128)(2,1)}), bf16[32,64,512]{2,1,0:T(8,128)(2,1)}) %all-gather.12.cloned.1.call-update) | async-done | bytes 2097168 | tf_op jit(solution)/shard_map/all_gather | solution.py:330
  103.5 1.9 %collective-permute-start.6 = (bf16[8,4,64,512]{3,2,1,0:T(8,128)(2,1)}, bf16[8,4,64,512]{3,2,1,0:T(8,128)(2,1)S(1)}, u32[]{:S(2)}, u32[]{:S(2)}) collective-permute-start(bf16[8,4,64,512]{3,2,1,0:T(8,128)(2,1)} %bitcast.19), channel_id=1, source_target_pairs={{0,8},{8,0},{16,24},{24,16},{32,40},{40,32},{48,56},{56,48},{64,72... | collective-permute-start | bytes 6291464 | tf_op jit(solution)/shard_map/ppermute | solution.py:346
  105.5 30.9 %all-gather.2 = bf16[896,512]{1,0:T(8,128)(2,1)} all-gather(bf16[112,512]{1,0:T(8,128)(2,1)} %get-tuple-element.28), channel_id=4, replica_groups=mesh['ctx'=64,'head'=8] {'head'}, dimensions={0}, use_global_device_ids=true | all-gather | bytes 1032192 | tf_op jit(solution)/shard_map/all_gather | solution.py:344
  136.3 9.5 %all-gather.10.cloned.1.call-done = bf16[1152,512]{1,0:T(8,128)(2,1)} async-done(((bf16[144,512]{1,0:T(8,128)(2,1)}), bf16[1152,512]{1,0:T(8,128)(2,1)}) %all-gather.10.cloned.1.call-update) | async-done | bytes 1179664 | tf_op jit(solution)/shard_map/all_gather | solution.py:344
  145.8 1.3 copy-done.2
  147.1 4.8 %output_product.1 = bf16[256,512]{1,0:T(8,128)(2,1)} custom-call(s32[5]{0:T(128)} %stack.56.side_ref, bf16[8,144,512]{2,1,0:T(8,128)(2,1)} %bitcast.21, bf16[8,112,512]{2,1,0:T(8,128)(2,1)} %bitcast.17, bf16[8,4,64,512]{3,2,1,0:T(8,128)(2,1)} %bitcast.20, bf16[8,4,64,512]{3,2,1,0:T(8,128)(2,1)} %copy-done.2), custom_call_target="tpu_custom_call" | custom-call | flops 1073741824 | bytes 6291456 | tf_op jit(solution)/shard_map/output_product/pallas_call | solution.py:174
  (25 shorter events, 7.1 us)
Async XLA Ops:
  6.5 51.2 %all-gather.8.cloned.1.call-start = ((), (), s32[]{:S(2)}) async-start(), calls=%async_computation.2 | async-start | bytes 2359296 | tf_op jit(solution)/shard_map/all_gather | solution.py:321
  8.9 28.9 %all-to-all-start = ((bf16[8,64,512]{2,1,0:T(8,128)(2,1)}), bf16[8,64,512]{2,1,0:T(8,128)(2,1)S(1)}, u32[]{:S(2)}, u32[]{:S(2)}) async-start(bf16[8,64,512]{2,1,0:T(8,128)(2,1)} %broadcast_in_dim.9), calls=%async_computation | async-start | bytes 1048576 | tf_op jit(solution)/shard_map/all_to_all | solution.py:325
  19.3 43.0 %collective-permute-start.3 = (bf16[2048,512]{1,0:T(8,128)(2,1)}, bf16[2048,512]{1,0:T(8,128)(2,1)}, u32[]{:S(2)}, u32[]{:S(2)}) collective-permute-start(bf16[2048,512]{1,0:T(8,128)(2,1)} %ko_ref.1), channel_id=1, source_target_pairs={{0,8},{8,0},{16,24},{24,16},{32,40},{40,32},{48,56},{56,48},{64,72... | collective-permute-start | bytes 6291464 | tf_op jit(solution)/shard_map/ppermute | solution.py:322
  21.2 41.0 %collective-permute-start.4 = (bf16[2048,512]{1,0:T(8,128)(2,1)}, bf16[2048,512]{1,0:T(8,128)(2,1)}, u32[]{:S(2)}, u32[]{:S(2)}) collective-permute-start(bf16[2048,512]{1,0:T(8,128)(2,1)} %vo_ref.1), channel_id=1, source_target_pairs={{0,8},{8,0},{16,24},{24,16},{32,40},{40,32},{48,56},{56,48},{64,72... | collective-permute-start | bytes 6291464 | tf_op jit(solution)/shard_map/ppermute | solution.py:323
  23.6 10.4 %collective-permute-start.2 = (bf16[64,512]{1,0:T(8,128)(2,1)}, bf16[64,512]{1,0:T(8,128)(2,1)S(1)}, u32[]{:S(2)}, u32[]{:S(2)}) collective-permute-start(bf16[64,512]{1,0:T(8,128)(2,1)} %param.13), channel_id=1, source_target_pairs={{0,256},{8,264},{16,272},{24,280},{32,288},{40,296},{48,304},{56,3... | collective-permute-start | bytes 196616 | tf_op jit(solution)/shard_map/ppermute | solution.py:328
  26.9 7.6 %collective-permute-start.1 = (bf16[64,512]{1,0:T(8,128)(2,1)}, bf16[64,512]{1,0:T(8,128)(2,1)S(1)}, u32[]{:S(2)}, u32[]{:S(2)}) collective-permute-start(bf16[64,512]{1,0:T(8,128)(2,1)} %param.13), channel_id=1, source_target_pairs={{0,384},{8,392},{16,400},{24,408},{32,416},{40,424},{48,432},{56,4... | collective-permute-start | bytes 196616 | tf_op jit(solution)/shard_map/ppermute | solution.py:328
  28.9 7.3 %collective-permute-start = (bf16[64,512]{1,0:T(8,128)(2,1)}, bf16[64,512]{1,0:T(8,128)(2,1)S(1)}, u32[]{:S(2)}, u32[]{:S(2)}) collective-permute-start(bf16[64,512]{1,0:T(8,128)(2,1)} %param.13), channel_id=1, source_target_pairs={{0,128},{8,136},{16,144},{24,152},{32,160},{40,168},{48,176},{56,1... | collective-permute-start | bytes 196616 | tf_op jit(solution)/shard_map/ppermute | solution.py:328
  39.4 8.0 %copy-start.3 = (s32[32]{0:T(128)S(1)}, s32[32]{0:T(128)}, u32[]{:S(2)}) copy-start(s32[32]{0:T(128)} %param.15) | copy-start | bytes 388
  39.4 8.1 %copy-start.4 = (s32[32]{0:T(128)S(1)}, s32[32]{0:T(128)}, u32[]{:S(2)}) copy-start(s32[32]{0:T(128)} %param.14) | copy-start | bytes 388
  39.4 30.6 %all-to-all-start.1 = ((bf16[4,8,64,512]{3,2,1,0:T(8,128)(2,1)}), bf16[4,8,64,512]{3,2,1,0:T(8,128)(2,1)S(1)}, u32[]{:S(2)}, u32[]{:S(2)}) async-start(bf16[4,8,64,512]{3,2,1,0:T(8,128)(2,1)} %broadcast_in_dim.18), calls=%async_computation.1 | async-start | bytes 4194304 | tf_op jit(solution)/shard_map/all_to_all | solution.py:332
  46.6 56.9 %all-gather.12.cloned.1.call-start = ((), (), s32[]{:S(2)}) async-start(), calls=%async_computation.4 | async-start | bytes 2359296 | tf_op jit(solution)/shard_map/all_gather | solution.py:330
  47.4 98.4 %all-gather.10.cloned.1.call-start = ((), (), s32[]{:S(2)}) async-start(), calls=%async_computation.3 | async-start | bytes 1327104 | tf_op jit(solution)/shard_map/all_gather | solution.py:344
  70.0 6.0 %collective-permute-start.5 = (bf16[4,8,64,512]{3,2,1,0:T(8,128)(2,1)S(1)}, bf16[4,8,64,512]{3,2,1,0:T(8,128)(2,1)S(1)}, u32[]{:S(2)}, u32[]{:S(2)}) collective-permute-start(bf16[4,8,64,512]{3,2,1,0:T(8,128)(2,1)S(1)} %all-to-all-done.1.w_ref), channel_id=1, source_target_pairs={{0,8},{8,0},{16,24},{24,16},{32,40},{40,32},{48,56},{56,48},{64,72... | collective-permute-start | bytes 6291464 | tf_op jit(solution)/shard_map/ppermute | solution.py:339
  71.9 1.7 %copy-start = (bf16[2,8,256,256]{3,2,1,0:T(8,128)(2,1)S(1)}, bf16[2,8,256,256]{3,2,1,0:T(8,128)(2,1)}, u32[]{:S(2)}) copy-start(bf16[2,8,256,256]{3,2,1,0:T(8,128)(2,1)} %normalize.1.x_ref) | copy-start | bytes 6291460
  77.3 0.7 copy-start.1
  103.5 42.3 %collective-permute-start.6 = (bf16[8,4,64,512]{3,2,1,0:T(8,128)(2,1)}, bf16[8,4,64,512]{3,2,1,0:T(8,128)(2,1)S(1)}, u32[]{:S(2)}, u32[]{:S(2)}) collective-permute-start(bf16[8,4,64,512]{3,2,1,0:T(8,128)(2,1)} %bitcast.19), channel_id=1, source_target_pairs={{0,8},{8,0},{16,24},{24,16},{32,40},{40,32},{48,56},{56,48},{64,72... | collective-permute-start | bytes 6291464 | tf_op jit(solution)/shard_map/ppermute | solution.py:346
  145.8 1.3 copy-start.2
Sparse Core Ops, SparseCore 0:
  9.4 48.2 all-gather.7
  59.8 43.7 all-gather.11
  105.6 40.1 all-gather.9
